TPU v7x, 256 devices: a whole 4x4x8 slice. The times are simulated.
256 devices in a mesh: row: 8 (over x_hi, y), col: 32 (over z, x_lo, core).
Axes of the slice: x: 4 (x_hi: 2, x_lo: 2; x = x_hi * 2 + x_lo), y: 4, z: 8, core: 2. Of those that a mesh axis runs over, the one named last changes fastest.
Arguments:
- region_inverse: float32 [4096, 4096], P('row', 'col'), may hold values from -6 to 6
- factor_cols: float32 [3, 4096, 512], P(None, 'row'), may hold values from -0.09375 to 0.09375
- parent_factor: float32 [2, 512, 512], P(None, 'col'), may hold values from -0.25 to 0.25
- diag_inverse: float32 [3, 512, 512], P(None, 'col'), may hold values from -6 to 6
- listed: int32 [3, 8], replicated, may hold values from 0 to 1, as said below
Outputs:
- col_blocks: float32 [3, 4096, 512], P(None, ('row', 'col'))
- diag_blocks: float32 [3, 512, 512], P(None, 'col')
- parent_rows: float32 [2, 512, 512], P(None, 'col')
Inputs may be any that keep to these rules, and one draw needn't show every extreme that they name: listed[0] has exactly 6 ones; listed[1] and listed[2] have exactly 4 ones each, all at blocks that listed[0] also lists.
All inputs are finite; a program needn't handle non-finite values.
Results may differ from a plain program's by a relative error of at most 0.0001.
Values sent between devices are 32-bit elements; how exact they have to be, the bound alone decides.
A program may use at most 64 MiB of HBM per device.

v0:
```python
import jax
import jax.numpy as jnp
from jax import lax
from jax.sharding import PartitionSpec as P


def broadcast(value, axis, source):
    kept = jnp.where(lax.axis_index(axis) == source, value, 0).astype(value.dtype)
    return lax.psum(kept, axis)


def matmul_plain(left, right):
    return jnp.dot(left, right, precision=lax.Precision.HIGHEST, preferred_element_type=jnp.float32)


def matmul_left(left, right):
    return lax.dot_general(
        left,
        right,
        (((0,), (0,)), ((), ())),
        precision=lax.Precision.HIGHEST,
        preferred_element_type=jnp.float32,
    )


def row_weights(listed_row, first_row, count, width):
    global_rows = first_row + lax.iota(jnp.int32, count)
    block_ids = global_rows // width
    table = lax.iota(jnp.int32, listed_row.shape[0])
    hits = (block_ids[:, None] == table[None, :]).astype(jnp.float32) * listed_row.astype(
        jnp.float32
    )[None, :]
    return jnp.sum(hits, axis=1)


def total_sums(values):
    return lax.psum(tuple(values), ("row", "col"))


def shards(region_inverse, factor_cols, parent_factor, diag_inverse, listed):
    row_count = lax.axis_size("row")
    col_count = lax.axis_size("col")
    row_place = lax.axis_index("row")
    col_place = lax.axis_index("col")
    rows_here, cols_here = region_inverse.shape
    width = factor_cols.shape[2]
    group = rows_here // col_count
    ratio = col_count // row_count
    diag_width = width // col_count
    diag_start = col_place * diag_width
    full_diag, full_parent = (
        lax.all_gather(diag_inverse, "col", axis=1, tiled=True),
        lax.all_gather(parent_factor, "col", axis=1, tiled=True),
    )
    masks = [
        row_weights(listed[member], row_place * rows_here, rows_here, width) for member in range(3)
    ]
    factors = [factor_cols[member] * masks[member][:, None] for member in range(3)]
    group_masks = [
        lax.dynamic_slice_in_dim(masks[member], col_place * group, group, 0) for member in range(3)
    ]
    pieces = [
        lax.dynamic_slice_in_dim(factors[member], col_place * group, group, 0)
        for member in range(3)
    ]

    def column_pass(members, extra_rows):
        slices = [
            lax.dynamic_slice_in_dim(factors[member], col_place % ratio * cols_here, cols_here, 0)
            for member in members
        ]
        stacked = jnp.stack(slices, axis=1)
        received = broadcast(stacked, "row", col_place // ratio)
        right_side = received.reshape(cols_here, len(members) * width)
        summed = lax.psum_scatter(
            matmul_plain(region_inverse, right_side), "col", scatter_dimension=0, tiled=True
        )
        outputs = []
        terms = []
        for place, member in enumerate(members):
            partial_sum = summed
            if extra_rows[place] is not None:
                partial_sum = partial_sum + extra_rows[place]
            column = -partial_sum * group_masks[member][:, None]
            outputs.append(column)
            terms.append(-matmul_left(pieces[member], column))
        return (outputs, terms)

    parent_out, parent_terms = column_pass([0], [None])
    parent_col = parent_out[0]
    parent_totals = total_sums(parent_terms)
    parent_diag = full_diag[0] + parent_totals[0]
    parent_slice = lax.dynamic_slice_in_dim(parent_diag, diag_start, diag_width, 0)
    links = [full_parent[0], full_parent[1]]
    extra_rows = [matmul_plain(parent_col, links[place]) for place in range(2)]
    extra_sums = [matmul_left(parent_col, pieces[place + 1]) for place in range(2)]
    child_cols = []
    diag_list = [parent_slice]
    upper_list = []
    for place in range(2):
        outputs, terms = column_pass([place + 1], [extra_rows[place]])
        child_cols.append(outputs[0])
        link_terms = [extra_sums[place]]
        places = [place]
        count = len(places)
        diags = []
        uppers = []
        totals = total_sums(list(terms) + list(link_terms))
        for k, finish_place in enumerate(places):
            link_cols = lax.dynamic_slice_in_dim(links[finish_place], diag_start, diag_width, 1)
            upper_total = totals[count + k]
            upper_slice = -(
                lax.dynamic_slice_in_dim(upper_total, diag_start, diag_width, 0)
                + matmul_plain(parent_slice, links[finish_place])
            )
            weighted_diag = matmul_left(link_cols, parent_diag)
            link_upper = -(
                matmul_left(link_cols, upper_total)
                + matmul_plain(weighted_diag, links[finish_place])
            )
            diag_rows = lax.dynamic_slice_in_dim(
                full_diag[finish_place + 1], diag_start, diag_width, 0
            )
            total_rows = lax.dynamic_slice_in_dim(totals[k], diag_start, diag_width, 0)
            diags.append(diag_rows + total_rows - link_upper)
            uppers.append(upper_slice)
        diags, uppers = (diags, uppers)
        diag_list = diag_list + diags
        upper_list = upper_list + uppers
    col_blocks = jnp.stack([parent_col] + child_cols)
    diag_blocks = jnp.stack(diag_list)
    parent_rows = jnp.stack(upper_list)
    return (col_blocks, diag_blocks, parent_rows)


def solution(mesh):
    in_specs = (
        P("row", "col"),
        P(None, "row", None),
        P(None, "col", None),
        P(None, "col", None),
        P(),
    )
    out_specs = (P(None, ("row", "col"), None), P(None, "col", None), P(None, "col", None))
    return jax.shard_map(shards, mesh=mesh, in_specs=in_specs, out_specs=out_specs, check_vma=False)
```

profile of v0, /device:TPU:1, one launch (start us, length us, event | category | flops | bytes accessed | tf_op | source)
XLA Modules:
  0.0 894.3 jit_solution(15378608520947166456)
XLA Ops:
  7.2 0.0 copy-start
  7.2 0.0 all-reduce.7.cloned.1.call-start
  7.3 0.8 convert_bitcast_fusion.2
  8.1 0.1 select_reduce_fusion.1
  8.2 2.1 bitcast_multiply_fusion.1
  10.3 0.0 copy-start.4
  10.3 0.0 copy-start.5
  10.3 0.0 copy-start.3
  10.3 0.8 dynamic-slice_select_fusion.2
  11.2 0.2 copy-done.4
  11.4 0.9 dynamic-slice_select_fusion
  12.3 0.0 copy-done.5
  12.3 0.0 all-reduce.7.cloned.1.call-update
  12.3 0.0 reduce-scatter.10.cloned.1.call-start
  12.3 90.1 %all-reduce.7.cloned.1.call-done = (f32[128,512]{1,0:T(8,128)}, f32[128,512]{1,0:T(8,128)}, f32[128,512]{1,0:T(8,128)}) async-done(((f32[128,512]{1,0:T(8,128)}, f32[128,512]{1,0:T(8,128)}, f32[128,512]{1,0:T(8,128)}), (f32[128,512]{1,0:T(8,128)}, f32[128,512]{1,0:T(8,128)}, f32[128,512]{1,0:T(8,128)})) %all-reduce.7.cloned.1.call-update) | async-done | bytes 786448 | tf_op jit(solution)/shard_map/psum | solution.py:9
  102.5 2.0 convolution_bitcast_fusion.2
  104.5 1.4 copy.17
  105.9 0.0 reduce-scatter.10.cloned.1.call-update
  105.9 0.0 reduce-scatter.12.cloned.1.call-start
  106.0 1.0 convolution_bitcast_fusion.1
  107.0 1.3 copy.19
  108.3 0.0 reduce-scatter.12.cloned.1.call-update
  108.4 0.0 all-gather.3.cloned.1.call-start
  108.4 0.5 all-gather.3.cloned.1.call-update
  108.9 0.0 reduce-scatter.14.cloned.1.call-start
  109.0 1.0 convolution_bitcast_fusion
  110.0 1.3 copy.21
  111.4 0.0 reduce-scatter.14.cloned.1.call-update
  111.4 0.0 all-gather.5.cloned.1.call-start
  111.4 0.5 all-gather.5.cloned.1.call-update
  112.0 0.2 all-reduce.5.cloned.1.call-start
  112.2 0.1 dynamic_slice.63
  112.3 0.1 dynamic_slice.65
  112.4 0.1 dynamic_slice.67
  112.4 112.2 %reduce-scatter.10.cloned.1.call-done = f32[16,512]{1,0:T(8,128)} async-done(((f32[512,512]{1,0:T(8,128)}), f32[16,512]{1,0:T(8,128)}) %reduce-scatter.10.cloned.1.call-update) | async-done | bytes 32784
  224.7 0.9 copy.18
  225.5 2.9 convolution_negate_fusion.2
  228.4 2.0 fusion.33
  230.4 2.7 fusion.34
  233.1 110.6 %reduce-scatter.12.cloned.1.call-done = f32[16,512]{1,0:T(8,128)} async-done(((f32[512,512]{1,0:T(8,128)}), f32[16,512]{1,0:T(8,128)}) %reduce-scatter.12.cloned.1.call-update) | async-done | bytes 32784 | tf_op jit(solution)/shard_map/reduce_scatter | solution.py:75
  343.8 68.3 %all-gather.3.cloned.1.call-done = f32[2,512,512]{2,1,0:T(8,128)} async-done(((f32[2,16,512]{2,1,0:T(8,128)}), f32[2,512,512]{2,1,0:T(8,128)}) %all-gather.3.cloned.1.call-update) | async-done | bytes 2097168 | tf_op jit(solution)/shard_map/all_gather | solution.py:53
  412.1 2.0 fusion.13
  414.1 2.8 convolution_negate_fusion.1
  416.9 111.7 %reduce-scatter.14.cloned.1.call-done = f32[16,512]{1,0:T(8,128)} async-done(((f32[512,512]{1,0:T(8,128)}), f32[16,512]{1,0:T(8,128)}) %reduce-scatter.14.cloned.1.call-update) | async-done | bytes 32784 | tf_op jit(solution)/shard_map/reduce_scatter | solution.py:75
  528.5 1.4 fusion.11
  529.9 2.9 convolution_negate_fusion
  532.8 0.0 all-reduce.5.cloned.1.call-update
  532.8 0.1 copy.16
  532.9 0.7 pad_maximum_fusion
  533.6 1.2 fusion.64
  534.7 63.3 %all-gather.5.cloned.1.call-done = f32[3,512,512]{2,1,0:T(8,128)} async-done(((f32[3,16,512]{2,1,0:T(8,128)}), f32[3,512,512]{2,1,0:T(8,128)}) %all-gather.5.cloned.1.call-update) | async-done | bytes 3145744 | tf_op jit(solution)/shard_map/all_gather | solution.py:52
  598.0 3.0 fusion.63
  601.0 276.3 %all-reduce.5.cloned.1.call-done = (f32[512,512]{1,0:T(8,128)}, f32[512,512]{1,0:T(8,128)}, f32[512,512]{1,0:T(8,128)}, f32[512,512]{1,0:T(8,128)}, f32[512,512]{1,0:T(8,128)}) async-done(((f32[512,512]{1,0:T(8,128)}, f32[512,512]{1,0:T(8,128)}, f32[512,512]{1,0:T(8,128)}, f32[512,512]{1,0:T(8,128)}, f32[512,512]{1,0:T(8,128)}), (f32[512,512]{1,0:T(8,128)}, f32[512,512]{1,0:T(8,128)}, f32[512,512]{1,0:T(8,128)}, ...) | async-done | bytes 5242896 | tf_op jit(solution)/shard_map/psum | solution.py:37
  877.4 1.9 fusion.14
  879.3 0.7 fusion.25
  880.0 0.7 fusion.27
  880.7 0.7 fusion.21
  881.4 0.7 fusion.23
  882.1 0.6 fusion.3
  882.7 0.6 fusion.1
  883.3 0.6 pad_maximum_fusion.2
  884.0 1.4 fusion.9
  885.4 1.4 fusion.6
  886.8 0.6 pad_maximum_fusion.1
  (17 shorter events, 0.1 us)
Async XLA Ops:
  7.2 95.3 %copy-start = (f32[512,128]{1,0:T(8,128)S(1)}, f32[512,128]{1,0:T(8,128)}, u32[]{:S(2)}) copy-start(f32[512,128]{1,0:T(8,128)} %param.5) | copy-start | bytes 786436
  7.2 95.3 %all-reduce.7.cloned.1.call-start = ((), (), s32[]{:S(2)}) async-start(), calls=%async_computation.9 | async-start | bytes 1572864 | tf_op jit(solution)/shard_map/psum | solution.py:9
  10.3 1.1 copy-start.4
  10.3 2.0 copy-start.5
  10.3 218.1 %copy-start.3 = (f32[512,512]{1,0:T(8,128)}, f32[512,512]{1,0:T(8,128)S(1)}, u32[]{:S(2)}) copy-start(f32[512,512]{1,0:T(8,128)S(1)} %get-tuple-element.21) | copy-start | bytes 3145732
  12.3 212.4 %reduce-scatter.10.cloned.1.call-start = ((), (), s32[]{:S(2)}) async-start(), calls=%async_computation.5 | async-start | bytes 1081344
  102.5 3.5 copy-start.9
  105.9 237.8 %reduce-scatter.12.cloned.1.call-start = ((), (), s32[]{:S(2)}) async-start(), calls=%async_computation.6 | async-start | bytes 1081344 | tf_op jit(solution)/shard_map/reduce_scatter | solution.py:75
  106.0 3.0 copy-start.8
  108.4 303.7 %all-gather.3.cloned.1.call-start = ((), (), s32[]{:S(2)}) async-start(), calls=%async_computation.3 | async-start | bytes 2162688 | tf_op jit(solution)/shard_map/all_gather | solution.py:53
  108.9 419.6 %reduce-scatter.14.cloned.1.call-start = ((), (), s32[]{:S(2)}) async-start(), calls=%async_computation.7 | async-start | bytes 1081344 | tf_op jit(solution)/shard_map/reduce_scatter | solution.py:75
  111.4 486.6 %all-gather.5.cloned.1.call-start = ((), (), s32[]{:S(2)}) async-start(), calls=%async_computation.4 | async-start | bytes 3244032 | tf_op jit(solution)/shard_map/all_gather | solution.py:52
  112.0 765.4 %all-reduce.5.cloned.1.call-start = ((), (), s32[]{:S(2)}) async-start(), calls=%async_computation.8 | async-start | bytes 10485760 | tf_op jit(solution)/shard_map/psum | solution.py:37
  412.1 116.4 %copy-start.1 = (f32[2,512,512]{2,1,0:T(8,128)S(1)}, f32[2,512,512]{2,1,0:T(8,128)}, u32[]{:S(2)}) copy-start(f32[2,512,512]{2,1,0:T(8,128)} %all-gather.3.cloned.1.call-done) | copy-start | bytes 6291460
  877.4 1.9 copy-start.2
  877.4 2.6 copy-start.7
  879.3 2.1 copy-start.6
Sparse Core Ops, SparseCore 0:
  12.4 90.0 all-reduce.6
  106.0 118.5 reduce-scatter.9
  227.2 116.5 reduce-scatter.11
  345.5 66.5 all-gather.2
  414.4 114.0 reduce-scatter.13
  530.3 67.7 all-gather.4
  604.3 273.0 all-reduce.4
where the time goes:
time: 895 us; the launch traced here: 894 us
  waiting for transfers between devices  834 us (93%)
  matrix products  27.4 us (3%)
  between operations  14.3 us (2%)
  local copies, waits for them, and re-layouts  9.69 us (1%)
    psum x1, waiting for transfers between devices, total_sums(): return lax.psum(tuple(values), ('row', 'col'))  276 us
    reduce_scatter x2, waiting for transfers between devices, column_pass(): lax.psum_scatter(matmul_plain(region_inverse, right_side), 'col', scatter...  222 us
    unnamed x8, waiting for transfers between devices  113 us
    psum x1, waiting for transfers between devices, broadcast(): return lax.psum(kept, axis)  90.1 us
    all_gather x1, waiting for transfers between devices, shards(): lax.all_gather(parent_factor, 'col', axis=1, tiled=True)  68.3 us
    all_gather x1, waiting for transfers between devices, shards(): lax.all_gather(diag_inverse, 'col', axis=1, tiled=True)  63.3 us
  transfers between devices with their start and end apart: 7, of which 7 were waited for; matrix products, arithmetic and copies ran while one was open for 3% of the time, Pallas kernels for 0%

commit v1 on v0

v1 whole, which is shorter than its diff:
```python
import functools

import jax
import jax.numpy as jnp
from jax import lax
from jax.experimental import pallas as pl
from jax.experimental.pallas import tpu as pltpu
from jax.sharding import PartitionSpec as P

MESH = pl.DeviceIdType.MESH
HIGH = lax.Precision.HIGHEST

S_A, S_FS, S_FA, S_G, S_GN, S_D, S_RB, S_Y0, S_YO, S_YU, S_TR, S_ZM, S_ZB, S_WM, S_WB, S_UO, S_GZ, S_ZO = range(0, 54, 3)
N_SEM = 54


def mm(a, b):
    return jnp.dot(a, b, precision=HIGH, preferred_element_type=jnp.float32)


def mm_t(a, b):
    return lax.dot_general(
        a, b, (((0,), (0,)), ((), ())), precision=HIGH, preferred_element_type=jnp.float32
    )


def kernel(
    R, C, W, planes,
    a_ref, f_ref, g_ref, d_ref, listed_ref,
    col_ref, diag_ref, par_ref,
    abuf, fb, pb, rb, gc, gn, db, y0n, yc, yo, yu, tp, tpw, tr, trw, ts, tsw,
    zm, zb, wm, wb, eb, uo, ge, gz, zp, zo, send, recv, sendx,
):
    Q = C // R
    NQ, HZ, GC = W // Q, W // R, W // C
    SP = HZ // R
    HW = NQ // HZ
    r = lax.axis_index("row")
    c = lax.axis_index("col")
    z = c // Q
    q = c % Q

    def flip(row, place):
        return 2 * ((place // 2 + row // (R // 2)) % 2) + place % 2

    n = flip(r, q)
    partner = (z + R // 2) % R
    n_cols = pl.ds(pl.multiple_of(n * NQ, NQ), NQ)
    my_rows = pl.ds(pl.multiple_of(z * HZ, HZ), HZ)

    def push(src, dst, s, row, col, k=0):
        pltpu.make_async_remote_copy(
            src_ref=src, dst_ref=dst, send_sem=send.at[s + k], recv_sem=recv.at[s + k],
            device_id=(row, col), device_id_type=MESH,
        ).start()

    def arrived(view, s, k=0):
        pltpu.make_async_copy(view, view, recv.at[s + k]).wait()

    def sent(view, s, k=0):
        pltpu.make_async_copy(view, view, send.at[s + k]).wait()

    def weight(member, block):
        return listed_ref[member, block].astype(jnp.float32)

    barrier = pltpu.get_barrier_semaphore()

    @pl.loop(1, C)
    def _(k):
        pl.semaphore_signal(barrier, inc=1, device_id=(r, (c + k) % C), device_id_type=MESH)

    @pl.loop(1, R)
    def _(k):
        for place in range(Q):
            pl.semaphore_signal(
                barrier, inc=1, device_id=((r + k) % R, z * Q + place), device_id_type=MESH
            )

    pl.semaphore_wait(barrier, C - 1 + (R - 1) * Q)

    def piece(i):
        return pl.ds(pl.multiple_of(i * HZ, HZ), HZ)

    @pl.when(r == z)
    def _():
        for j in range(3):
            for k in range(1, R):
                i = (z + k) % R
                push(
                    f_ref.at[j, piece(i), n_cols], fb.at[j, piece(i)], S_FS, i, z * Q + flip(i, n), j
                )
            push(
                f_ref.at[j, piece(z), n_cols], fb.at[j, piece(z)], S_FS,
                partner, z * Q + flip(partner, n), j,
            )

    a_cols = pl.ds(pl.multiple_of(q * NQ, NQ), NQ)
    for k in range(1, Q):
        push(a_ref, abuf.at[:, a_cols], S_A, r, z * Q + (q + k) % Q)

    g_rows = pl.ds(pl.multiple_of(c * GC, GC), GC)
    n_rows = pl.ds(pl.multiple_of(q * GC, GC), GC)

    @pl.loop(1, C)
    def _(k):
        other = (c + k) % C
        share = flip(r, other % Q)
        push(
            g_ref.at[:, :, pl.ds(pl.multiple_of(share * NQ, NQ), NQ)], gc.at[:, g_rows], S_G, r, other
        )

    for k in range(1, Q):
        push(g_ref, gn.at[:, n_rows], S_GN, r, z * Q + (q + k) % Q)
        push(d_ref.at[0], db.at[n_rows], S_D, r, z * Q + (q + k) % Q)

    abuf[:, a_cols] = a_ref[...]
    gc[:, g_rows] = g_ref[:, :, n_cols]
    gn[:, n_rows] = g_ref[...]
    db[n_rows] = d_ref[0]

    @pl.when(r == z)
    def _():
        for j in range(3):
            fb[j] = f_ref[j, :, n_cols]

    @pl.when(r != z)
    def _():
        for j in range(3):
            @pl.when(r == partner)
            def _():
                arrived(fb.at[j, : 2 * HZ], S_FS, j)

            @pl.when(r != partner)
            def _():
                arrived(fb.at[j, :HZ], S_FS, j)

            for k in range(1, R):
                i = (r + k) % R

                @pl.when(i != z)
                def _():
                    push(fb.at[j, piece(r)], fb.at[j, piece(r)], S_FA, i, z * Q + flip(i, n), j)

                    @pl.when(r == partner)
                    def _():
                        pltpu.make_async_remote_copy(
                            src_ref=fb.at[j, piece(z)], dst_ref=fb.at[j, piece(z)],
                            send_sem=sendx.at[0], recv_sem=recv.at[S_FA + j],
                            device_id=(i, z * Q + flip(i, n)), device_id_type=MESH,
                        ).start()

    arrived(abuf.at[:, : (Q - 1) * NQ], S_A)

    for j in range(3):
        @pl.when((r != z) & (r != partner))
        def _():
            arrived(fb.at[j, : (R - 1) * HZ], S_FA, j)

        @pl.when(r == partner)
        def _():
            arrived(fb.at[j, : (R - 2) * HZ], S_FA, j)

        pb[j] = mm(abuf[...], fb[j]) * weight(j, z)
        for k in range(1, R):
            other = (z + k) % R
            push(
                pb.at[j, piece(other)], rb.at[j, R - 1 - k], S_RB, r, other * Q + q, j
            )

    def summed(j):
        arrived(rb.at[j], S_RB, j)
        total = pb[j, my_rows]
        for k in range(R - 1):
            total = total + rb[j, k]
        return total

    def to_unit(j, plane):
        @pl.when(z != plane)
        def _():
            push(yc.at[j], yu.at[my_rows], S_YU, r, plane * Q + q, j)

        @pl.when(z == plane)
        def _():
            yu[my_rows] = yc[j]

    yc[0] = -weight(0, r) * summed(0)
    for k in range(1, Q):
        push(yc.at[0], y0n.at[:, n_cols], S_Y0, r, z * Q + (q + k) % Q)
    for plane in planes[:3]:
        to_unit(0, plane)
    y0n[:, n_cols] = yc[0]
    arrived(y0n.at[:, : (Q - 1) * NQ], S_Y0)
    col_ref[0] = y0n[n_rows]
    arrived(gc.at[:, : (C - 1) * GC], S_G)

    for j in (1, 2):
        cross = mm(y0n[...], gc[j - 1])
        yc[j] = -weight(j, r) * (summed(j) + cross)
        to_unit(j, planes[2 + j])
        for k in range(1, Q):
            other = (q + k) % Q
            push(
                yc.at[j, pl.ds(pl.multiple_of(other * GC, GC), GC)], yo.at[j - 1, :, n_cols],
                S_YO, r, z * Q + other,
            )
        yo[j - 1, :, n_cols] = yc[j, n_rows]

    def rows_sum(unit, member, source):
        @pl.when(z == planes[unit])
        def _():
            arrived(yu.at[: (R - 1) * HZ], S_YU, source)
            if unit in (1, 2):
                tpw[...] = (mm_t(yu[...], f_ref[member]) * weight(member, r)).reshape(HW, R, SP, W)
                for k in range(1, R):
                    i = (r + k) % R
                    push(tpw.at[:, i], trw.at[R - 1 - k], S_TR, i, z * Q + flip(i, n))
            else:
                tp[...] = mm_t(f_ref[member], yu[...]).reshape(R, R, SP, NQ)
                for k in range(1, R):
                    i = (r + k) % R
                    push(tp.at[:, i], tr.at[R - 1 - k], S_TR, i, z * Q + flip(i, n))

    rows_sum(0, 0, 0)
    rows_sum(1, 1, 0)
    rows_sum(2, 2, 0)
    rows_sum(3, 1, 1)
    rows_sum(4, 2, 2)

    def spread(unit, place):
        @pl.when(z == planes[unit])
        def _():
            if unit in (1, 2):
                arrived(trw, S_TR)
                total = tpw[:, r]
                for k in range(R - 1):
                    total = total + trw[k]
                tsw[...] = total
                for h in range(HW):
                    dest = n * HW + h

                    @pl.when(dest != z)
                    def _():
                        push(tsw.at[h], wm.at[unit - 1], S_WM, r, dest * Q + q, unit - 1)

                    @pl.when(dest == z)
                    def _():
                        wm[unit - 1] = tsw[h]
            else:
                arrived(tr, S_TR)
                total = tp[:, r]
                for k in range(R - 1):
                    total = total + tr[k]
                ts[...] = total
                for k in range(1, R):
                    dest = (z + k) % R
                    push(ts.at[dest], zm.at[place], S_ZM, r, dest * Q + q, place)
                zm[place] = ts[z]

    spread(0, 0)
    spread(1, 0)
    spread(2, 0)
    spread(3, 1)
    spread(4, 2)

    s_rows = pl.ds(pl.multiple_of(r * SP, SP), SP)
    flat = r * Q + q

    @pl.when(z != planes[0])
    def _():
        arrived(zm.at[0], S_ZM, 0)

    @pl.loop(1, C)
    def _(k):
        other = (flat + k) % C
        push(zm.at[0], zb.at[s_rows, n_cols], S_ZB, other // Q, z * Q + other % Q)

    zb[s_rows, n_cols] = zm[0]

    holds_w = z // HW == n

    @pl.when(holds_w)
    def _():
        for child in range(2):
            @pl.when(z != planes[1 + child])
            def _():
                arrived(wm.at[child], S_WM, child)

            @pl.loop(1, C)
            def _(k):
                other = (flat + k) % C
                share = flip(other // Q, other % Q)
                push(
                    wm.at[child, :, pl.ds(pl.multiple_of(share * NQ, NQ), NQ)],
                    wb.at[child, s_rows], S_WB, other // Q, z * Q + other % Q, child,
                )

            wb[child, s_rows] = wm[child, :, n_cols]

    arrived(db.at[: (Q - 1) * GC], S_D)
    arrived(gn.at[:, : (Q - 1) * GC], S_GN)
    arrived(fb.at[0, : (C - 1) * SP], S_ZB)
    zb[...] = db[...] - zb[...]
    diag_ref[0] = zb[n_rows]
    for child in range(2):
        @pl.when(holds_w)
        def _():
            arrived(wb.at[child, : (R - 1) * SP], S_WB, child)

        @pl.when(jnp.logical_not(holds_w))
        def _():
            arrived(wb.at[child], S_WB, child)

        eb[child] = wb[child] + mm(zb[...], gc[child])
        ge[child] = mm_t(gn[child], eb[child]).reshape(R, R, SP, NQ)
        for k in range(1, R):
            dest = (z + k) % R
            push(ge.at[child, dest, r], gz.at[child, R - 1 - k], S_GZ, r, dest * Q + q, child)
        for k in range(1, Q):
            other = (q + k) % Q
            push(
                eb.at[child, pl.ds(pl.multiple_of(other * GC, GC), GC)], uo.at[child, :, n_cols],
                S_UO, r, z * Q + other,
            )
        uo[child, :, n_cols] = eb[child, n_rows]

    o_rows = pl.ds(pl.multiple_of(r % (R // Q) * SP, SP), SP)
    o_place = r // (R // Q)
    for child in range(2):
        @pl.when(z != planes[3 + child])
        def _():
            arrived(zm.at[1 + child], S_ZM, 1 + child)

        arrived(gz.at[child], S_GZ, child)
        total = ge[child, z, r] - zm[1 + child]
        for k in range(R - 1):
            total = total + gz[child, k]
        zp[child] = total
        for k in range(1, R):
            push(
                zp.at[child], zo.at[child, o_rows, n_cols], S_ZO, (r + k) % R, z * Q + o_place, child
            )

        @pl.when(q == o_place)
        def _():
            zo[child, o_rows, n_cols] = zp[child]

        @pl.when(q != o_place)
        def _():
            push(zp.at[child], zo.at[child, o_rows, n_cols], S_ZO, r, z * Q + o_place, child)

    arrived(yo.at[:, :, : (Q - 1) * NQ], S_YO)
    col_ref[1:3] = yo[...]
    arrived(uo.at[:, :, : (Q - 1) * NQ], S_UO)
    par_ref[...] = -uo[...]
    for child in range(2):
        @pl.when(q == o_place)
        def _():
            arrived(rb.at[child, 0, : (R - 1) * SP], S_ZO, child)

        @pl.when(q != o_place)
        def _():
            arrived(rb.at[child, 0, : R * SP], S_ZO, child)

        diag_ref[1 + child] = d_ref[1 + child] + zo[child]

    sent(abuf.at[:, : (Q - 1) * NQ], S_A)
    sent(gc.at[:, : (C - 1) * GC], S_G)
    sent(gn.at[:, : (Q - 1) * GC], S_GN)
    sent(db.at[: (Q - 1) * GC], S_D)
    sent(y0n.at[:, : (Q - 1) * NQ], S_Y0)
    sent(yo.at[:, :, : (Q - 1) * NQ], S_YO)
    sent(uo.at[:, :, : (Q - 1) * NQ], S_UO)
    sent(fb.at[0, : (C - 1) * SP], S_ZB)
    for j in range(3):
        @pl.when(r == z)
        def _():
            sent(fb.at[j], S_FS, j)

        @pl.when(r != z)
        def _():
            sent(fb.at[j, : (R - 2) * HZ], S_FA, j)

        sent(rb.at[j], S_RB, j)

    @pl.when(r == partner)
    def _():
        pltpu.make_async_copy(
            fb.at[:, : (R - 2) * HZ], fb.at[:, : (R - 2) * HZ], sendx.at[0]
        ).wait()

    for j in range(3):
        targets = planes[:3] if j == 0 else planes[2 + j : 3 + j]
        inside = functools.reduce(jnp.logical_or, [z == plane for plane in targets])

        @pl.when(inside)
        def _():
            if len(targets) > 1:
                sent(yu.at[: (len(targets) - 1) * HZ], S_YU, j)

        @pl.when(jnp.logical_not(inside))
        def _():
            sent(yu.at[: len(targets) * HZ], S_YU, j)

    for unit in range(5):
        @pl.when(z == planes[unit])
        def _():
            if unit in (1, 2):
                sent(trw, S_TR)

                @pl.when(z // HW == n)
                def _():
                    if HW > 1:
                        sent(tsw.at[: HW - 1], S_WM, unit - 1)

                @pl.when(z // HW != n)
                def _():
                    sent(tsw, S_WM, unit - 1)
            else:
                place = (0, None, None, 1, 2)[unit]
                sent(tr, S_TR)
                sent(ts.at[: R - 1], S_ZM, place)

    for child in range(2):
        @pl.when(holds_w)
        def _():
            sent(fb.at[0, : (C - 1) * SP], S_WB, child)

        sent(gz.at[child], S_GZ, child)

        @pl.when(q == o_place)
        def _():
            sent(rb.at[child, 0, : (R - 1) * SP], S_ZO, child)

        @pl.when(q != o_place)
        def _():
            sent(rb.at[child, 0, : R * SP], S_ZO, child)


def shards(region_inverse, factor_cols, parent_factor, diag_inverse, listed):
    R = lax.axis_size("row")
    C = lax.axis_size("col")
    W = factor_cols.shape[2]
    Q = C // R
    NQ, HZ, GC = W // Q, W // R, W // C
    SP = HZ // R
    HW = NQ // HZ
    planes = (0, 2, 5, 3, 7)
    f32 = jnp.float32
    vmem = pl.BlockSpec(memory_space=pltpu.VMEM)
    smem = pl.BlockSpec(memory_space=pltpu.SMEM)
    scratch = [
        (W, W), (3, W, NQ), (3, W, NQ), (3, R - 1, HZ, NQ), (2, W, NQ), (2, HZ, W), (HZ, W),
        (HZ, W), (3, HZ, NQ), (2, GC, W), (W, NQ),
        (R, R, SP, NQ), (HW, R, SP, W), (R - 1, R, SP, NQ), (R - 1, HW, SP, W),
        (R, SP, NQ), (HW, SP, W),
        (3, SP, NQ), (HZ, W), (2, SP, W), (2, HZ, NQ), (2, HZ, NQ), (2, GC, W),
        (2, R, R, SP, NQ), (2, R - 1, SP, NQ), (2, SP, NQ), (2, GC, W),
    ]
    return pl.pallas_call(
        functools.partial(kernel, R, C, W, planes),
        out_shape=(
            jax.ShapeDtypeStruct((3, GC, W), f32),
            jax.ShapeDtypeStruct((3, GC, W), f32),
            jax.ShapeDtypeStruct((2, GC, W), f32),
        ),
        in_specs=[vmem, vmem, vmem, vmem, smem],
        out_specs=(vmem, vmem, vmem),
        scratch_shapes=[pltpu.VMEM(shape, f32) for shape in scratch]
        + [
            pltpu.SemaphoreType.DMA((N_SEM,)),
            pltpu.SemaphoreType.DMA((N_SEM,)),
            pltpu.SemaphoreType.DMA((1,)),
        ],
        compiler_params=pltpu.CompilerParams(collective_id=0, has_side_effects=True),
    )(region_inverse, factor_cols, parent_factor, diag_inverse, listed)


def solution(mesh):
    in_specs = (
        P("row", "col"),
        P(None, "row", None),
        P(None, "col", None),
        P(None, "col", None),
        P(),
    )
    out_specs = (P(None, ("row", "col"), None), P(None, "col", None), P(None, "col", None))
    return jax.shard_map(shards, mesh=mesh, in_specs=in_specs, out_specs=out_specs, check_vma=False)
```

time: 895 us -> 84.2 us (0.09)
  waiting for transfers between devices: 834 us -> 0 us
  Pallas kernels: 0 us -> 78.8 us
  matrix products: 27.4 us -> 0 us
  between operations: 14.3 us -> 0.64 us
    psum x2 -> x0, waiting for transfers between devices: 366 us -> none  [the longest x1 276 us: total_sums(): return lax.psum(tuple(values), ('row', 'col'))]
    reduce_scatter x2 -> x0, waiting for transfers between devices: 222 us -> none  [column_pass(): lax.psum_scatter(matmul_plain(region_inverse, right_side), 'col', scatter...]
    all_gather x2 -> x0, waiting for transfers between devices: 132 us -> none  [the longest x1 68.3 us: shards(): lax.all_gather(parent_factor, 'col', axis=1, tiled=True)]
    unnamed x8 -> x0, waiting for transfers between devices: 113 us -> none
    pallas_call x0 -> x1, Pallas kernels: none -> 78.8 us  [shards(): pl.pallas_call(functools.partial(kernel, R, C, W, planes), out_shape=(jax...]
    dot_general x18 -> x0, matrix products: 27.4 us -> none  [the longest x9 16 us: matmul_left(): lax.dot_general(left, right, (((0,), (0,)), ((), ())), precision=lax.Prec...]
  transfers between devices with their start and end apart: 7 -> 0, of which waited for: 7 -> 0; matrix products, arithmetic and copies ran while one was open for 3% -> 0% of each run, Pallas kernels for 0% -> 0%
where the time goes in v1:
time: 84.2 us; the launch traced here: 84 us
  Pallas kernels  78.8 us (94%)
  local copies, waits for them, and re-layouts  4.55 us (5%)
    pallas_call x1, Pallas kernels, shards(): pl.pallas_call(functools.partial(kernel, R, C, W, planes), out_shape=(jax...  78.8 us
    unnamed x3, local copies, waits for them, and re-layouts  4.55 us

profile of v1, /device:TPU:1, one launch (start us, length us, event | category | flops | bytes accessed | tf_op | source)
XLA Modules:
  0.0 84.0 jit_solution(8345409263585666254)
XLA Ops:
  0.6 78.8 %shard_map.76 = (f32[3,16,512]{2,1,0:T(8,128)}, f32[3,16,512]{2,1,0:T(8,128)}, f32[2,16,512]{2,1,0:T(8,128)}) custom-call(f32[512,128]{1,0:T(8,128)} %a_ref.1, f32[3,512,512]{2,1,0:T(8,128)} %f_ref.1, f32[2,16,512]{2,1,0:T(8,128)} %g_ref.1, f32[3,16,512]{2,1,0:T(8,128)} %d_ref.1, s32[3,8]{1,0:T(4,128)} %listed_ref.1), custom_call_target="tpu_custom_call" | custom-call | tf_op jit(solution)/shard_map/pallas_call | solution.py:459
  79.4 1.5 %copy.11 = f32[3,16,512]{2,1,0:T(8,128)} copy(f32[3,16,512]{2,1,0:T(8,128)} %get-tuple-element.6) | data formatting | bytes 196608
  81.0 1.5 %copy.12 = f32[3,16,512]{2,1,0:T(8,128)} copy(f32[3,16,512]{2,1,0:T(8,128)} %get-tuple-element.7) | data formatting | bytes 196608
  82.5 1.5 %copy.13 = f32[2,16,512]{2,1,0:T(8,128)} copy(f32[2,16,512]{2,1,0:T(8,128)} %get-tuple-element.8) | data formatting | bytes 131072

commit v2 on v1

v2 whole, which is shorter than its diff:
```python
import functools

import jax
import jax.numpy as jnp
from jax import lax
from jax.experimental import pallas as pl
from jax.experimental.pallas import tpu as pltpu
from jax.sharding import PartitionSpec as P

MESH = pl.DeviceIdType.MESH
HIGH = lax.Precision.HIGHEST

SIZES = dict(
    A=3, FS=3, FA=3, GN=1, D=1, GP=4, GM=3, X=3, RB=3, Y0=1, YO=1, YU=3, TR=1, ZM=3, ZB=1, WM=2, WB=2,
    UO=1, GZ=2, ZO=2, FX=1, FB=3, FV=1,
)
BASE = {}
N_SEM = 0
for _name, _size in SIZES.items():
    BASE[_name] = N_SEM
    N_SEM += _size

OFFSET = {1: 0, 3: 0, 4: 0, 2: -1, 7: -1, 5: 1, 6: 1}


def mm(a, b):
    return jnp.dot(a, b, precision=HIGH, preferred_element_type=jnp.float32)


def mm_t(a, b):
    return lax.dot_general(
        a, b, (((0,), (0,)), ((), ())), precision=HIGH, preferred_element_type=jnp.float32
    )


def kernel(
    R, C, W, planes,
    a_ref, f_ref, g_ref, d_ref, listed_ref,
    out_ref,
    abuf, fb, fv, pb, xb, rl, rb, gc, gn, db, y0n, yc, xc, yo, yu, tp, tpw, tr, trw, ts, tsw,
    zm, zb, wm, wb, eb, uo, ge, gz, zp, zo, send, recv,
):
    Q = C // R
    NQ, HZ, GC = W // Q, W // R, W // C
    SP = HZ // R
    HW = NQ // HZ
    HR = R // 2
    r = lax.axis_index("row")
    c = lax.axis_index("col")
    z = c // Q
    q = c % Q

    def flip(row, place):
        return 2 * ((place // 2 + row // HR) % 2) + place % 2

    def at(row, k):
        return (row // HR + k // HR) % 2 * HR + (row % HR + k % HR) % HR

    n = flip(r, q)
    partner = at(z, HR)
    core = q % 2
    sibling = q + 1 - 2 * core
    across = (q + 2) % Q
    n_cols = pl.ds(pl.multiple_of(n * NQ, NQ), NQ)

    def piece(i):
        return pl.ds(pl.multiple_of(i * HZ, HZ), HZ)

    my_rows = piece(z)

    def push(src, dst, s, row, col, k=0):
        s = BASE[s] + k
        pltpu.make_async_remote_copy(
            src_ref=src, dst_ref=dst, send_sem=send.at[s], recv_sem=recv.at[s],
            device_id=(row, col), device_id_type=MESH,
        ).start()

    def arrived(view, s, k=0):
        pltpu.make_async_copy(view, view, recv.at[BASE[s] + k]).wait()

    def sent(view, s, k=0):
        pltpu.make_async_copy(view, view, send.at[BASE[s] + k]).wait()

    def weight(member, block):
        return listed_ref[member, block].astype(jnp.float32)

    barrier = pltpu.get_barrier_semaphore()

    def greet(row, col):
        pl.semaphore_signal(barrier, inc=1, device_id=(row, col), device_id_type=MESH)

    for k in range(1, R):
        i = at(r, k)
        greet(i, z * Q + flip(i, n))
    for k in range(1, R):
        greet(r, (z + k) % R * Q + q)
    for k in range(1, Q):
        greet(r, z * Q + (q + k) % Q)
    for k, offset in OFFSET.items():
        if offset:
            @pl.when(at(z, k) == r)
            def _():
                greet(z, (z + offset) % R * Q + flip(z, n))

    near = z == r
    above = z == (r + 1) % R
    below = (z + 1) % R == r
    peers = 2 * (R - 1) + Q - 1

    @pl.when(above | below)
    def _():
        pl.semaphore_wait(barrier, peers + 2)

    @pl.when(jnp.logical_not(above | below))
    def _():
        pl.semaphore_wait(barrier, peers)

    for offset, here in ((0, near), (1, above), (-1, below)):
        @pl.when(here)
        def _():
            for j in range(3):
                for k, source in OFFSET.items():
                    if source == offset:
                        i = at(r, k)
                        push(
                            f_ref.at[j, piece(i), n_cols], fb.at[j, piece(i)], "FS",
                            i, r * Q + flip(i, n), j,
                        )
                if offset == 0:
                    push(
                        f_ref.at[j, piece(z), n_cols], fb.at[j, piece(z)], "FS",
                        partner, z * Q + flip(partner, n), j,
                    )

    a_cols = pl.ds(pl.multiple_of(q * NQ, NQ), NQ)
    x_cols = pl.ds(pl.multiple_of(across * NQ, NQ), NQ)
    push(a_ref, abuf.at[:, a_cols], "A", r, z * Q + across, 1)
    push(a_ref, abuf.at[:, a_cols], "A", r, z * Q + sibling, 0)
    keep = pltpu.make_async_copy(f_ref, fv, recv.at[BASE["FV"]])

    @pl.when(near)
    def _():
        for j in range(3):
            pltpu.make_async_copy(f_ref.at[j, :, n_cols], fb.at[j], recv.at[BASE["FB"] + j]).start()

    keep.start()

    n_rows = pl.ds(pl.multiple_of(q * GC, GC), GC)
    for k in range(1, Q):
        push(g_ref, gn.at[:, n_rows], "GN", r, z * Q + (q + k) % Q)
        push(d_ref.at[0], db.at[n_rows], "D", r, z * Q + (q + k) % Q)
    abuf[:, a_cols] = a_ref[...]
    gn[:, n_rows] = g_ref[...]
    db[n_rows] = d_ref[0]

    def forward(j):
        @pl.when(r != z)
        def _():
            @pl.when(r == partner)
            def _():
                arrived(fb.at[j, : 2 * HZ], "FS", j)

            @pl.when(r != partner)
            def _():
                arrived(fb.at[j, :HZ], "FS", j)

            for k in range(1, R):
                i = at(r, k)

                @pl.when(i != z)
                def _():
                    push(fb.at[j, piece(r)], fb.at[j, piece(r)], "FA", i, z * Q + flip(i, n), j)

                    @pl.when(r == partner)
                    def _():
                        pltpu.make_async_remote_copy(
                            src_ref=fb.at[j, piece(z)], dst_ref=fb.at[j, piece(z)],
                            send_sem=send.at[BASE["FX"]], recv_sem=recv.at[BASE["FA"] + j],
                            device_id=(i, z * Q + flip(i, n)), device_id_type=MESH,
                        ).start()

    def g_step(k):
        if k == 0:
            arrived(gn.at[:, : (Q - 1) * GC], "GN")
            gc[:, my_rows] = gn[:, :, n_cols]
        up = gn.at[:, :, n_cols] if k == 0 else gc.at[:, piece((z - k) % R)]
        down = gn.at[:, :, n_cols] if k == 0 else gc.at[:, piece((z + k) % R)]
        if k:
            arrived(up, "GP", k - 1)
        push(up, gc.at[:, piece((z - k) % R)], "GP", r, (z + 1) % R * Q + q, k)
        if k < R - 1 - HR:
            if k:
                arrived(down, "GM", k - 1)
            push(down, gc.at[:, piece((z + k) % R)], "GM", r, (z - 1) % R * Q + q, k)

    s = 1 - 2 * core

    def along(k):
        return (z + s * k) % R

    def product(j):
        @pl.when(r == z)
        def _():
            pltpu.make_async_copy(fb.at[j], fb.at[j], recv.at[BASE["FB"] + j]).wait()

        @pl.when((r != z) & (r != partner))
        def _():
            arrived(fb.at[j, : (R - 1) * HZ], "FA", j)

        @pl.when(r == partner)
        def _():
            arrived(fb.at[j, : (R - 2) * HZ], "FA", j)

        pb[j] = mm(abuf[...], fb[j]) * weight(j, z)

        def part(k):
            return pb.at[j, piece(along(k))]

        push(part(4), xb.at[j, 0], "X", r, along(2) * Q + q, j)
        push(part(3), xb.at[j, 1], "X", r, along(1) * Q + q, j)
        push(part(-3), xb.at[j, 2], "X", r, along(-1) * Q + q, j)
        push(part(1), rb.at[j, 0], "RB", r, along(1) * Q + q, j)
        push(part(-1), rb.at[j, 1], "RB", r, along(-1) * Q + q, j)

    def relay(j):
        arrived(xb.at[j], "X", j)
        rl[j, 0] = pb[j, piece(along(2))] + xb[j, 0] + xb[j, 1]
        rl[j, 1] = pb[j, piece(along(-2))] + xb[j, 2]
        push(rl.at[j, 0], rb.at[j, 2], "RB", r, along(2) * Q + q, j)
        push(rl.at[j, 1], rb.at[j, 3], "RB", r, along(-2) * Q + q, j)

    forward(0)
    forward(1)
    arrived(abuf.at[:, x_cols], "A", 1)
    push(abuf.at[:, x_cols], abuf.at[:, x_cols], "A", r, z * Q + sibling, 2)
    forward(2)
    g_step(0)
    arrived(abuf.at[:, a_cols], "A", 0)
    arrived(abuf.at[:, a_cols], "A", 2)
    product(0)
    g_step(1)
    product(1)
    relay(0)
    product(2)
    relay(1)
    g_step(2)
    relay(2)
    g_step(3)

    def summed(j):
        arrived(rb.at[j], "RB", j)
        return ((pb[j, my_rows] + rb[j, 0]) + (rb[j, 1] + rb[j, 2])) + rb[j, 3]

    def to_unit(j, plane):
        @pl.when(z != plane)
        def _():
            push(yc.at[j], yu.at[my_rows], "YU", r, plane * Q + q, j)

        @pl.when(z == plane)
        def _():
            yu[my_rows] = yc[j]

    yc[0] = -weight(0, r) * summed(0)
    for k in range(1, Q):
        push(yc.at[0], y0n.at[:, n_cols], "Y0", r, z * Q + (q + k) % Q)
    for plane in planes[:3]:
        to_unit(0, plane)
    y0n[:, n_cols] = yc[0]
    arrived(y0n.at[:, : (Q - 1) * NQ], "Y0")
    out_ref[0] = y0n[n_rows]
    arrived(gc.at[:, piece((z - HR) % R)], "GP", HR - 1)
    arrived(gc.at[:, piece((z + HR - 1) % R)], "GM", HR - 2)
    for j in (1, 2):
        xc[j - 1] = mm(y0n[...], gc[j - 1])

    def child_columns(j):
        yc[j] = -weight(j, r) * (summed(j) + xc[j - 1])
        to_unit(j, planes[2 + j])
        for k in range(1, Q):
            other = (q + k) % Q
            push(
                yc.at[j, pl.ds(pl.multiple_of(other * GC, GC), GC)], yo.at[j - 1, :, n_cols],
                "YO", r, z * Q + other,
            )
        yo[j - 1, :, n_cols] = yc[j, n_rows]

    def rows_sum(unit, member, source):
        @pl.when(z == planes[unit])
        def _():
            arrived(yu.at[: (R - 1) * HZ], "YU", source)
            if unit in (1, 2):
                tpw[...] = (mm_t(yu[...], fv[member]) * weight(member, r)).reshape(HW, R, SP, W)
                for k in range(1, R):
                    i = (r + k) % R
                    push(tpw.at[:, i], trw.at[R - 1 - k], "TR", i, z * Q + flip(i, n))
            else:
                tp[...] = mm_t(fv[member], yu[...]).reshape(R, R, SP, NQ)
                for k in range(1, R):
                    i = (r + k) % R
                    push(tp.at[:, i], tr.at[R - 1 - k], "TR", i, z * Q + flip(i, n))


    def spread(unit, place):
        @pl.when(z == planes[unit])
        def _():
            if unit in (1, 2):
                arrived(trw, "TR")
                total = tpw[:, r]
                for k in range(R - 1):
                    total = total + trw[k]
                tsw[...] = total
                for h in range(HW):
                    dest = n * HW + h

                    @pl.when(dest != z)
                    def _():
                        push(tsw.at[h], wm.at[unit - 1], "WM", r, dest * Q + q, unit - 1)

                    @pl.when(dest == z)
                    def _():
                        wm[unit - 1] = tsw[h]
            else:
                arrived(tr, "TR")
                total = tp[:, r]
                for k in range(R - 1):
                    total = total + tr[k]
                ts[...] = total
                for k in range(1, R):
                    dest = (z + k) % R
                    push(ts.at[dest], zm.at[place], "ZM", r, dest * Q + q, place)
                zm[place] = ts[z]

    keep.wait()
    rows_sum(0, 0, 0)
    rows_sum(1, 1, 0)
    rows_sum(2, 2, 0)
    child_columns(1)
    spread(0, 0)
    spread(1, 0)
    spread(2, 0)
    child_columns(2)

    s_rows = pl.ds(pl.multiple_of(r * SP, SP), SP)
    flat = r * Q + q

    @pl.when(z != planes[0])
    def _():
        arrived(zm.at[0], "ZM", 0)

    @pl.loop(1, C)
    def _(k):
        other = (flat + k) % C
        push(zm.at[0], zb.at[s_rows, n_cols], "ZB", other // Q, z * Q + other % Q)

    zb[s_rows, n_cols] = zm[0]

    holds_w = z // HW == n

    @pl.when(holds_w)
    def _():
        for child in range(2):
            @pl.when(z != planes[1 + child])
            def _():
                arrived(wm.at[child], "WM", child)

            @pl.loop(1, C)
            def _(k):
                other = (flat + k) % C
                share = flip(other // Q, other % Q)
                push(
                    wm.at[child, :, pl.ds(pl.multiple_of(share * NQ, NQ), NQ)],
                    wb.at[child, s_rows], "WB", other // Q, z * Q + other % Q, child,
                )

            wb[child, s_rows] = wm[child, :, n_cols]

    rows_sum(3, 1, 1)
    rows_sum(4, 2, 2)
    arrived(db.at[: (Q - 1) * GC], "D")
    arrived(fb.at[0, : (C - 1) * SP], "ZB")
    zb[...] = db[...] - zb[...]
    out_ref[3] = zb[n_rows]
    for child in range(2):
        @pl.when(holds_w)
        def _():
            arrived(wb.at[child, : (R - 1) * SP], "WB", child)

        @pl.when(jnp.logical_not(holds_w))
        def _():
            arrived(wb.at[child], "WB", child)

        eb[child] = wb[child] + mm(zb[...], gc[child])
        ge[child] = mm_t(gn[child], eb[child]).reshape(R, R, SP, NQ)
        for k in range(1, R):
            dest = (z + k) % R
            push(ge.at[child, dest, r], gz.at[child, R - 1 - k], "GZ", r, dest * Q + q, child)
        for k in range(1, Q):
            other = (q + k) % Q
            push(
                eb.at[child, pl.ds(pl.multiple_of(other * GC, GC), GC)], uo.at[child, :, n_cols],
                "UO", r, z * Q + other,
            )
        uo[child, :, n_cols] = eb[child, n_rows]

    spread(3, 1)
    spread(4, 2)

    o_rows = pl.ds(pl.multiple_of(r % (R // Q) * SP, SP), SP)
    o_place = r // (R // Q)
    for child in range(2):
        @pl.when(z != planes[3 + child])
        def _():
            arrived(zm.at[1 + child], "ZM", 1 + child)

        arrived(gz.at[child], "GZ", child)
        total = ge[child, z, r] - zm[1 + child]
        for k in range(R - 1):
            total = total + gz[child, k]
        zp[child] = total
        for k in range(1, R):
            push(
                zp.at[child], zo.at[child, o_rows, n_cols], "ZO", (r + k) % R, z * Q + o_place, child
            )

        @pl.when(q == o_place)
        def _():
            zo[child, o_rows, n_cols] = zp[child]

        @pl.when(q != o_place)
        def _():
            push(zp.at[child], zo.at[child, o_rows, n_cols], "ZO", r, z * Q + o_place, child)

    arrived(yo.at[:, :, : (Q - 1) * NQ], "YO")
    out_ref[1:3] = yo[...]
    arrived(uo.at[:, :, : (Q - 1) * NQ], "UO")
    out_ref[6:8] = -uo[...]
    for child in range(2):
        @pl.when(q == o_place)
        def _():
            arrived(rb.at[child, 0, : (R - 1) * SP], "ZO", child)

        @pl.when(q != o_place)
        def _():
            arrived(rb.at[child, 0, : R * SP], "ZO", child)

        out_ref[4 + child] = d_ref[1 + child] + zo[child]

    sent(a_ref, "A", 0)
    sent(a_ref, "A", 1)
    sent(a_ref, "A", 2)
    for k in range(HR):
        sent(gc.at[:, my_rows], "GP", k)
    for k in range(R - 1 - HR):
        sent(gc.at[:, my_rows], "GM", k)
    sent(gn.at[:, : (Q - 1) * GC], "GN")
    sent(db.at[: (Q - 1) * GC], "D")
    sent(y0n.at[:, : (Q - 1) * NQ], "Y0")
    sent(yo.at[:, :, : (Q - 1) * NQ], "YO")
    sent(uo.at[:, :, : (Q - 1) * NQ], "UO")
    sent(fb.at[0, : (C - 1) * SP], "ZB")
    for j in range(3):
        @pl.when(near)
        def _():
            sent(fb.at[j, : 4 * HZ], "FS", j)

        @pl.when(above | below)
        def _():
            sent(fb.at[j, : 2 * HZ], "FS", j)

        @pl.when(r != z)
        def _():
            sent(fb.at[j, : (R - 2) * HZ], "FA", j)

        sent(xb.at[j], "X", j)
        sent(rb.at[j], "RB", j)

    @pl.when(r == partner)
    def _():
        sent(fb.at[:, : (R - 2) * HZ], "FX")

    for j in range(3):
        targets = planes[:3] if j == 0 else planes[2 + j : 3 + j]
        inside = functools.reduce(jnp.logical_or, [z == plane for plane in targets])

        @pl.when(inside)
        def _():
            if len(targets) > 1:
                sent(yu.at[: (len(targets) - 1) * HZ], "YU", j)

        @pl.when(jnp.logical_not(inside))
        def _():
            sent(yu.at[: len(targets) * HZ], "YU", j)

    for unit in range(5):
        @pl.when(z == planes[unit])
        def _():
            if unit in (1, 2):
                sent(trw, "TR")

                @pl.when(z // HW == n)
                def _():
                    if HW > 1:
                        sent(tsw.at[: HW - 1], "WM", unit - 1)

                @pl.when(z // HW != n)
                def _():
                    sent(tsw, "WM", unit - 1)
            else:
                place = (0, None, None, 1, 2)[unit]
                sent(tr, "TR")
                sent(ts.at[: R - 1], "ZM", place)

    for child in range(2):
        @pl.when(holds_w)
        def _():
            sent(fb.at[0, : (C - 1) * SP], "WB", child)

        sent(gz.at[child], "GZ", child)

        @pl.when(q == o_place)
        def _():
            sent(rb.at[child, 0, : (R - 1) * SP], "ZO", child)

        @pl.when(q != o_place)
        def _():
            sent(rb.at[child, 0, : R * SP], "ZO", child)


def shards(region_inverse, factor_cols, parent_factor, diag_inverse, listed):
    R = lax.axis_size("row")
    C = lax.axis_size("col")
    W = factor_cols.shape[2]
    Q = C // R
    NQ, HZ, GC = W // Q, W // R, W // C
    SP = HZ // R
    HW = NQ // HZ
    planes = (0, 2, 5, 3, 7)
    f32 = jnp.float32
    vmem = pl.BlockSpec(memory_space=pltpu.VMEM)
    smem = pl.BlockSpec(memory_space=pltpu.SMEM)
    scratch = [
        (W, W), (3, W, NQ), (3, W, W), (3, W, NQ), (3, 3, HZ, NQ), (3, 2, HZ, NQ), (3, 4, HZ, NQ),
        (2, W, NQ), (2, HZ, W), (HZ, W), (HZ, W), (3, HZ, NQ), (2, HZ, NQ), (2, GC, W), (W, NQ),
        (R, R, SP, NQ), (HW, R, SP, W), (R - 1, R, SP, NQ), (R - 1, HW, SP, W),
        (R, SP, NQ), (HW, SP, W),
        (3, SP, NQ), (HZ, W), (2, SP, W), (2, HZ, NQ), (2, HZ, NQ), (2, GC, W),
        (2, R, R, SP, NQ), (2, R - 1, SP, NQ), (2, SP, NQ), (2, GC, W),
    ]
    whole = pl.pallas_call(
        functools.partial(kernel, R, C, W, planes),
        out_shape=jax.ShapeDtypeStruct((8, GC, W), f32),
        in_specs=[vmem, pl.BlockSpec(memory_space=pl.ANY), vmem, vmem, smem],
        out_specs=vmem,
        scratch_shapes=[pltpu.VMEM(shape, f32) for shape in scratch]
        + [pltpu.SemaphoreType.DMA((N_SEM,)), pltpu.SemaphoreType.DMA((N_SEM,))],
        compiler_params=pltpu.CompilerParams(
            collective_id=0, has_side_effects=True, vmem_limit_bytes=24 * 2**20
        ),
    )(region_inverse, factor_cols, parent_factor, diag_inverse, listed)
    return pl.pallas_call(
        split,
        out_shape=(
            jax.ShapeDtypeStruct((3, GC, W), f32),
            jax.ShapeDtypeStruct((3, GC, W), f32),
            jax.ShapeDtypeStruct((2, GC, W), f32),
        ),
        in_specs=[vmem],
        out_specs=(vmem, vmem, vmem),
        compiler_params=pltpu.CompilerParams(vmem_limit_bytes=4 * 2**20),
    )(whole)


def split(whole_ref, col_ref, diag_ref, par_ref):
    col_ref[...] = whole_ref[0:3]
    diag_ref[...] = whole_ref[3:6]
    par_ref[...] = whole_ref[6:8]


def solution(mesh):
    in_specs = (
        P("row", "col"),
        P(None, "row", None),
        P(None, "col", None),
        P(None, "col", None),
        P(),
    )
    out_specs = (P(None, ("row", "col"), None), P(None, "col", None), P(None, "col", None))
    return jax.shard_map(shards, mesh=mesh, in_specs=in_specs, out_specs=out_specs, check_vma=False)
```

time: 84.2 us -> 85.5 us (1.015)
    unnamed x3 -> x10, local copies, waits for them, and re-layouts: 4.55 us -> 5.24 us
    pallas_call x1 -> x2, Pallas kernels: 78.8 us -> 79 us  [the longest x1 78.3 us: shards(): pl.pallas_call(functools.partial(kernel, R, C, W, planes), out_shape=jax....]
where the time goes in v2:
time: 85.5 us; the launch traced here: 84.9 us
  Pallas kernels  79 us (92%)
  local copies, waits for them, and re-layouts  5.24 us (6%)
    pallas_call x1, Pallas kernels, shards(): pl.pallas_call(functools.partial(kernel, R, C, W, planes), out_shape=jax....  78.3 us
    unnamed x10, local copies, waits for them, and re-layouts  5.24 us

profile of v2, /device:TPU:1, one launch (start us, length us, event | category | flops | bytes accessed | tf_op | source)
XLA Modules:
  0.0 84.9 jit_solution(12385140256545313103)
XLA Ops:
  0.6 0.0 copy-start
  0.6 1.9 %copy-done = f32[3,512,512]{2,1,0:T(8,128)S(1)} copy-done((f32[3,512,512]{2,1,0:T(8,128)S(1)}, f32[3,512,512]{2,1,0:T(8,128)}, u32[]{:S(2)}) %copy-start) | copy-done | bytes 3145752
  2.5 0.0 copy-start.1
  2.5 0.9 %copy-done.1 = f32[512,128]{1,0:T(8,128)S(1)} copy-done((f32[512,128]{1,0:T(8,128)S(1)}, f32[512,128]{1,0:T(8,128)}, u32[]{:S(2)}) %copy-start.1) | copy-done | bytes 262168
  3.5 0.0 copy-start.2
  3.5 0.9 %copy-done.2 = f32[3,16,512]{2,1,0:T(8,128)S(1)} copy-done((f32[3,16,512]{2,1,0:T(8,128)S(1)}, f32[3,16,512]{2,1,0:T(8,128)}, u32[]{:S(2)}) %copy-start.2) | copy-done | bytes 98328
  4.4 0.0 copy-start.3
  4.4 0.8 copy-done.3
  5.2 0.0 copy-start.4
  5.2 0.7 copy-done.4
  5.9 78.3 %shard_map.76.whole_ref = f32[8,16,512]{2,1,0:T(8,128)S(1)} custom-call(f32[512,128]{1,0:T(8,128)S(1)} %copy-done.1, f32[3,512,512]{2,1,0:T(8,128)S(1)} %copy-done, f32[2,16,512]{2,1,0:T(8,128)S(1)} %copy-done.3, f32[3,16,512]{2,1,0:T(8,128)S(1)} %copy-done.2, s32[3,8]{1,0:T(4,128)S(1)} %copy-done.4), custom_call_target="tpu_custom_call" | custom-call | tf_op jit(solution)/shard_map/pallas_call | solution.py:549
  84.2 0.7 shard_map.77
Async XLA Ops:
  0.6 1.9 %copy-start = (f32[3,512,512]{2,1,0:T(8,128)S(1)}, f32[3,512,512]{2,1,0:T(8,128)}, u32[]{:S(2)}) copy-start(f32[3,512,512]{2,1,0:T(8,128)} %f_ref.1) | copy-start | bytes 9437188
  2.5 0.9 %copy-start.1 = (f32[512,128]{1,0:T(8,128)S(1)}, f32[512,128]{1,0:T(8,128)}, u32[]{:S(2)}) copy-start(f32[512,128]{1,0:T(8,128)} %a_ref.1) | copy-start | bytes 786436
  3.5 0.9 %copy-start.2 = (f32[3,16,512]{2,1,0:T(8,128)S(1)}, f32[3,16,512]{2,1,0:T(8,128)}, u32[]{:S(2)}) copy-start(f32[3,16,512]{2,1,0:T(8,128)} %d_ref.1) | copy-start | bytes 294916
  4.4 0.8 copy-start.3
  5.2 0.7 copy-start.4

commit v3 on v2

--- a/solution.py
+++ b/solution.py
@@ -11,8 +11,8 @@
 HIGH = lax.Precision.HIGHEST
 
 SIZES = dict(
-    A=3, FS=3, FA=3, GN=1, D=1, GP=4, GM=3, X=3, RB=3, Y0=1, YO=1, YU=3, TR=1, ZM=3, ZB=1, WM=2, WB=2,
-    UO=1, GZ=2, ZO=2, FX=1, FB=3, FV=1,
+    A=3, FS=3, FA=3, FX=1, GN=1, G0=1, D=1, GP=4, GM=3, X=3, RB=3, Y0=1, YO=1, YU=3, ZM=3, ZB=1, WM=2,
+    WB=2, UO=1, GZ=2, ZO=2, FB=3, FV=1, LA=1, LG=1, LC=1, LD=1,
 )
 BASE = {}
 N_SEM = 0
@@ -23,8 +23,24 @@
 OFFSET = {1: 0, 3: 0, 4: 0, 2: -1, 7: -1, 5: 1, 6: 1}
 
 
+def halves(x):
+    hi = x.astype(jnp.bfloat16)
+    return hi, (x - hi.astype(jnp.float32)).astype(jnp.bfloat16)
+
+
+def dot(a, b, dims=((1,), (0,))):
+    return lax.dot_general(a, b, (dims, ((), ())), preferred_element_type=jnp.float32)
+
+
+def mm3(a_hi, a_lo, b):
+    b_hi, b_lo = halves(b)
+    cols = b.shape[1]
+    both = dot(a_hi, jnp.concatenate([b_hi, b_lo], axis=1))
+    return both[:, :cols] + (both[:, cols:] + dot(a_lo, b_hi))
+
+
 def mm(a, b):
-    return jnp.dot(a, b, precision=HIGH, preferred_element_type=jnp.float32)
+    return mm3(*halves(a), b)
 
 
 def mm_t(a, b):
@@ -37,8 +53,8 @@
     R, C, W, planes,
     a_ref, f_ref, g_ref, d_ref, listed_ref,
     out_ref,
-    abuf, fb, fv, pb, xb, rl, rb, gc, gn, db, y0n, yc, xc, yo, yu, tp, tpw, tr, trw, ts, tsw,
-    zm, zb, wm, wb, eb, uo, ge, gz, zp, zo, send, recv,
+    abuf, fb, fv, pb, xb, rl, rb, gc, gn, db, dv, y0n, yc, xc, yo, yu, tp, tpw, zr, wr,
+    zm, zb, wm, wb, eb, uo, ge, gz, zp, zo, ah, al, fh, fl, send, recv,
 ):
     Q = C // R
     NQ, HZ, GC = W // Q, W // R, W // C
@@ -105,6 +121,45 @@
     near = z == r
     above = z == (r + 1) % R
     below = (z + 1) % R == r
+    a_cols = pl.ds(pl.multiple_of(q * NQ, NQ), NQ)
+    x_cols = pl.ds(pl.multiple_of(across * NQ, NQ), NQ)
+    n_rows = pl.ds(pl.multiple_of(q * GC, GC), GC)
+    g_rows = pl.ds(pl.multiple_of(c * GC, GC), GC)
+
+    def local(src, dst, s, k=0):
+        pltpu.make_async_copy(src, dst, recv.at[BASE[s] + k]).start()
+
+    def loaded(view, s, k=0):
+        pltpu.make_async_copy(view, view, recv.at[BASE[s] + k]).wait()
+
+    for unit, member in enumerate((0, 1, 2, 1, 2)):
+        @pl.when(z == planes[unit])
+        def _():
+            local(f_ref.at[member], fv, "FV")
+
+    local(g_ref.at[:, :, n_cols], gc.at[:, g_rows], "LC")
+    local(a_ref, abuf.at[:, a_cols], "LA")
+
+    @pl.when(near)
+    def _():
+        for j in range(3):
+            local(f_ref.at[j, :, n_cols], fb.at[j], "FB", j)
+
+    local(g_ref, gn.at[:, n_rows], "LG")
+    local(d_ref, dv, "LD")
+    in_cols = functools.reduce(jnp.logical_or, [z == planes[unit] for unit in (0, 3, 4)])
+    in_rows = functools.reduce(jnp.logical_or, [z == planes[unit] for unit in (1, 2)])
+
+    @pl.when(in_cols)
+    def _():
+        loaded(fv, "FV")
+        fh[...], fl[...] = halves(fv[...].T)
+
+    @pl.when(in_rows)
+    def _():
+        loaded(fv, "FV")
+        fh[...], fl[...] = halves(fv[...])
+
     peers = 2 * (R - 1) + Q - 1
 
     @pl.when(above | below)
@@ -132,26 +187,15 @@
                         partner, z * Q + flip(partner, n), j,
                     )
 
-    a_cols = pl.ds(pl.multiple_of(q * NQ, NQ), NQ)
-    x_cols = pl.ds(pl.multiple_of(across * NQ, NQ), NQ)
+    for k in range(1, Q):
+        other = (q + k) % Q
+        share = flip(r, other)
+        push(
+            g_ref.at[:, :, pl.ds(pl.multiple_of(share * NQ, NQ), NQ)], gc.at[:, g_rows], "G0",
+            r, z * Q + other,
+        )
     push(a_ref, abuf.at[:, a_cols], "A", r, z * Q + across, 1)
     push(a_ref, abuf.at[:, a_cols], "A", r, z * Q + sibling, 0)
-    keep = pltpu.make_async_copy(f_ref, fv, recv.at[BASE["FV"]])
-
-    @pl.when(near)
-    def _():
-        for j in range(3):
-            pltpu.make_async_copy(f_ref.at[j, :, n_cols], fb.at[j], recv.at[BASE["FB"] + j]).start()
-
-    keep.start()
-
-    n_rows = pl.ds(pl.multiple_of(q * GC, GC), GC)
-    for k in range(1, Q):
-        push(g_ref, gn.at[:, n_rows], "GN", r, z * Q + (q + k) % Q)
-        push(d_ref.at[0], db.at[n_rows], "D", r, z * Q + (q + k) % Q)
-    abuf[:, a_cols] = a_ref[...]
-    gn[:, n_rows] = g_ref[...]
-    db[n_rows] = d_ref[0]
 
     def forward(j):
         @pl.when(r != z)
@@ -181,17 +225,17 @@
 
     def g_step(k):
         if k == 0:
-            arrived(gn.at[:, : (Q - 1) * GC], "GN")
-            gc[:, my_rows] = gn[:, :, n_cols]
-        up = gn.at[:, :, n_cols] if k == 0 else gc.at[:, piece((z - k) % R)]
-        down = gn.at[:, :, n_cols] if k == 0 else gc.at[:, piece((z + k) % R)]
+            loaded(gc.at[:, g_rows], "LC")
+            arrived(gc.at[:, : (Q - 1) * GC], "G0")
+        up = gc.at[:, piece((z - k) % R)]
+        down = gc.at[:, piece((z + k) % R)]
         if k:
             arrived(up, "GP", k - 1)
-        push(up, gc.at[:, piece((z - k) % R)], "GP", r, (z + 1) % R * Q + q, k)
+        push(up, up, "GP", r, (z + 1) % R * Q + q, k)
         if k < R - 1 - HR:
             if k:
                 arrived(down, "GM", k - 1)
-            push(down, gc.at[:, piece((z + k) % R)], "GM", r, (z - 1) % R * Q + q, k)
+            push(down, down, "GM", r, (z - 1) % R * Q + q, k)
 
     s = 1 - 2 * core
 
@@ -201,7 +245,7 @@
     def product(j):
         @pl.when(r == z)
         def _():
-            pltpu.make_async_copy(fb.at[j], fb.at[j], recv.at[BASE["FB"] + j]).wait()
+            loaded(fb.at[j], "FB", j)
 
         @pl.when((r != z) & (r != partner))
         def _():
@@ -211,7 +255,7 @@
         def _():
             arrived(fb.at[j, : (R - 2) * HZ], "FA", j)
 
-        pb[j] = mm(abuf[...], fb[j]) * weight(j, z)
+        pb[j] = mm3(ah[...], al[...], fb[j]) * weight(j, z)
 
         def part(k):
             return pb.at[j, piece(along(k))]
@@ -229,23 +273,27 @@
         push(rl.at[j, 0], rb.at[j, 2], "RB", r, along(2) * Q + q, j)
         push(rl.at[j, 1], rb.at[j, 3], "RB", r, along(-2) * Q + q, j)
 
+    g_step(0)
     forward(0)
+    g_step(1)
     forward(1)
+    g_step(2)
+    forward(2)
     arrived(abuf.at[:, x_cols], "A", 1)
     push(abuf.at[:, x_cols], abuf.at[:, x_cols], "A", r, z * Q + sibling, 2)
-    forward(2)
-    g_step(0)
+    loaded(abuf.at[:, a_cols], "LA")
+    for k in range(1, Q):
+        push(g_ref, gn.at[:, n_rows], "GN", r, z * Q + (q + k) % Q)
+        push(d_ref.at[0], db.at[n_rows], "D", r, z * Q + (q + k) % Q)
+    g_step(3)
     arrived(abuf.at[:, a_cols], "A", 0)
     arrived(abuf.at[:, a_cols], "A", 2)
+    ah[...], al[...] = halves(abuf[...])
     product(0)
-    g_step(1)
     product(1)
     relay(0)
     product(2)
     relay(1)
-    g_step(2)
-    relay(2)
-    g_step(3)
 
     def summed(j):
         arrived(rb.at[j], "RB", j)
@@ -266,6 +314,7 @@
     for plane in planes[:3]:
         to_unit(0, plane)
     y0n[:, n_cols] = yc[0]
+    relay(2)
     arrived(y0n.at[:, : (Q - 1) * NQ], "Y0")
     out_ref[0] = y0n[n_rows]
     arrived(gc.at[:, piece((z - HR) % R)], "GP", HR - 1)
@@ -284,84 +333,88 @@
             )
         yo[j - 1, :, n_cols] = yc[j, n_rows]
 
-    def rows_sum(unit, member, source):
+    def rows_sum(unit, source, place):
         @pl.when(z == planes[unit])
         def _():
             arrived(yu.at[: (R - 1) * HZ], "YU", source)
-            if unit in (1, 2):
-                tpw[...] = (mm_t(yu[...], fv[member]) * weight(member, r)).reshape(HW, R, SP, W)
-                for k in range(1, R):
-                    i = (r + k) % R
-                    push(tpw.at[:, i], trw.at[R - 1 - k], "TR", i, z * Q + flip(i, n))
-            else:
-                tp[...] = mm_t(fv[member], yu[...]).reshape(R, R, SP, NQ)
-                for k in range(1, R):
-                    i = (r + k) % R
-                    push(tp.at[:, i], tr.at[R - 1 - k], "TR", i, z * Q + flip(i, n))
-
-
-    def spread(unit, place):
+            tp[...] = mm3(fh[...], fl[...], yu[...]).reshape(R, R, SP, NQ)
+            zr[place, 0] = tp[z, r]
+
+            @pl.loop(1, R * R)
+            def _(t):
+                i = at(r, t // R)
+                dest = (z + t % R) % R
+                push(tp.at[dest, i], zr.at[place, t // R], "ZM", i, dest * Q + flip(i, n), place)
+
+    def cross_sum(unit, child):
         @pl.when(z == planes[unit])
         def _():
-            if unit in (1, 2):
-                arrived(trw, "TR")
-                total = tpw[:, r]
-                for k in range(R - 1):
-                    total = total + trw[k]
-                tsw[...] = total
-                for h in range(HW):
-                    dest = n * HW + h
-
-                    @pl.when(dest != z)
-                    def _():
-                        push(tsw.at[h], wm.at[unit - 1], "WM", r, dest * Q + q, unit - 1)
-
-                    @pl.when(dest == z)
-                    def _():
-                        wm[unit - 1] = tsw[h]
-            else:
-                arrived(tr, "TR")
-                total = tp[:, r]
-                for k in range(R - 1):
-                    total = total + tr[k]
-                ts[...] = total
-                for k in range(1, R):
-                    dest = (z + k) % R
-                    push(ts.at[dest], zm.at[place], "ZM", r, dest * Q + q, place)
-                zm[place] = ts[z]
-
-    keep.wait()
+            arrived(yu.at[: (R - 1) * HZ], "YU", 0)
+            y_hi, y_lo = halves(yu[...].T)
+            total = dot(y_hi, fh[...]) + (dot(y_hi, fl[...]) + dot(y_lo, fh[...]))
+            tpw[...] = (total * weight(1 + child, r)).reshape(HW, R, SP, W)
+
+            @pl.loop(0, R * HW)
+            def _(t):
+                i = at(r, t // HW)
+                dest = n * HW + t % HW
+                own = (t < HW) & (dest == z)
+
+                @pl.when(own)
+                def _():
+                    wr[child, 0] = tpw[t % HW, r]
+
+                @pl.when(jnp.logical_not(own))
+                def _():
+                    push(
+                        tpw.at[t % HW, i], wr.at[child, t // HW], "WM", i, dest * Q + flip(i, n), child
+                    )
+
+    def added(place, plane):
+        @pl.when(z == plane)
+        def _():
+            arrived(zr.at[place, : R - 1], "ZM", place)
+
+        @pl.when(z != plane)
+        def _():
+            arrived(zr.at[place], "ZM", place)
+
+        return functools.reduce(jnp.add, [zr[place, k] for k in range(R)])
+
     rows_sum(0, 0, 0)
-    rows_sum(1, 1, 0)
-    rows_sum(2, 2, 0)
+    cross_sum(1, 0)
+    cross_sum(2, 1)
     child_columns(1)
-    spread(0, 0)
-    spread(1, 0)
-    spread(2, 0)
     child_columns(2)
+    rows_sum(3, 1, 1)
+    rows_sum(4, 2, 2)
 
     s_rows = pl.ds(pl.multiple_of(r * SP, SP), SP)
     flat = r * Q + q
 
-    @pl.when(z != planes[0])
-    def _():
-        arrived(zm.at[0], "ZM", 0)
+    zm[...] = added(0, planes[0])
 
     @pl.loop(1, C)
     def _(k):
         other = (flat + k) % C
-        push(zm.at[0], zb.at[s_rows, n_cols], "ZB", other // Q, z * Q + other % Q)
-
-    zb[s_rows, n_cols] = zm[0]
+        push(zm, zb.at[s_rows, n_cols], "ZB", other // Q, z * Q + other % Q)
+
+    zb[s_rows, n_cols] = zm[...]
 
     holds_w = z // HW == n
 
     @pl.when(holds_w)
     def _():
         for child in range(2):
+            @pl.when(z == planes[1 + child])
+            def _():
+                arrived(wr.at[child, : R - 1], "WM", child)
+
             @pl.when(z != planes[1 + child])
             def _():
-                arrived(wm.at[child], "WM", child)
+                arrived(wr.at[child], "WM", child)
+
+            wm[child] = functools.reduce(jnp.add, [wr[child, k] for k in range(R)])
 
             @pl.loop(1, C)
             def _(k):
@@ -374,9 +427,11 @@
 
             wb[child, s_rows] = wm[child, :, n_cols]
 
-    rows_sum(3, 1, 1)
-    rows_sum(4, 2, 2)
+    loaded(dv, "LD")
+    loaded(gn.at[:, n_rows], "LG")
+    arrived(gn.at[:, : (Q - 1) * GC], "GN")
     arrived(db.at[: (Q - 1) * GC], "D")
+    db[n_rows] = dv[0]
     arrived(fb.at[0, : (C - 1) * SP], "ZB")
     zb[...] = db[...] - zb[...]
     out_ref[3] = zb[n_rows]
@@ -402,18 +457,12 @@
             )
         uo[child, :, n_cols] = eb[child, n_rows]
 
-    spread(3, 1)
-    spread(4, 2)
-
     o_rows = pl.ds(pl.multiple_of(r % (R // Q) * SP, SP), SP)
     o_place = r // (R // Q)
     for child in range(2):
-        @pl.when(z != planes[3 + child])
-        def _():
-            arrived(zm.at[1 + child], "ZM", 1 + child)
-
+        share = added(1 + child, planes[3 + child])
         arrived(gz.at[child], "GZ", child)
-        total = ge[child, z, r] - zm[1 + child]
+        total = ge[child, z, r] - share
         for k in range(R - 1):
             total = total + gz[child, k]
         zp[child] = total
@@ -443,11 +492,11 @@
         def _():
             arrived(rb.at[child, 0, : R * SP], "ZO", child)
 
-        out_ref[4 + child] = d_ref[1 + child] + zo[child]
-
-    sent(a_ref, "A", 0)
-    sent(a_ref, "A", 1)
-    sent(a_ref, "A", 2)
+        out_ref[4 + child] = dv[1 + child] + zo[child]
+
+    for k in range(3):
+        sent(abuf.at[:, a_cols], "A", k)
+    sent(gc.at[:, : (Q - 1) * GC], "G0")
     for k in range(HR):
         sent(gc.at[:, my_rows], "GP", k)
     for k in range(R - 1 - HR):
@@ -491,24 +540,19 @@
         def _():
             sent(yu.at[: len(targets) * HZ], "YU", j)
 
-    for unit in range(5):
+    for unit, place in ((0, 0), (3, 1), (4, 2)):
         @pl.when(z == planes[unit])
         def _():
-            if unit in (1, 2):
-                sent(trw, "TR")
-
-                @pl.when(z // HW == n)
-                def _():
-                    if HW > 1:
-                        sent(tsw.at[: HW - 1], "WM", unit - 1)
-
-                @pl.when(z // HW != n)
-                def _():
-                    sent(tsw, "WM", unit - 1)
-            else:
-                place = (0, None, None, 1, 2)[unit]
-                sent(tr, "TR")
-                sent(ts.at[: R - 1], "ZM", place)
+            sent(fb.at[0, : (R * R - 1) * SP], "ZM", place)
+
+    for child in range(2):
+        @pl.when((z == planes[1 + child]) & holds_w)
+        def _():
+            sent(fv.at[: (R * HW - 1) * SP], "WM", child)
+
+        @pl.when((z == planes[1 + child]) & jnp.logical_not(holds_w))
+        def _():
+            sent(fv.at[: R * HW * SP], "WM", child)
 
     for child in range(2):
         @pl.when(holds_w)
@@ -539,22 +583,23 @@
     vmem = pl.BlockSpec(memory_space=pltpu.VMEM)
     smem = pl.BlockSpec(memory_space=pltpu.SMEM)
     scratch = [
-        (W, W), (3, W, NQ), (3, W, W), (3, W, NQ), (3, 3, HZ, NQ), (3, 2, HZ, NQ), (3, 4, HZ, NQ),
-        (2, W, NQ), (2, HZ, W), (HZ, W), (HZ, W), (3, HZ, NQ), (2, HZ, NQ), (2, GC, W), (W, NQ),
-        (R, R, SP, NQ), (HW, R, SP, W), (R - 1, R, SP, NQ), (R - 1, HW, SP, W),
-        (R, SP, NQ), (HW, SP, W),
-        (3, SP, NQ), (HZ, W), (2, SP, W), (2, HZ, NQ), (2, HZ, NQ), (2, GC, W),
+        (W, W), (3, W, NQ), (W, W), (3, W, NQ), (3, 3, HZ, NQ), (3, 2, HZ, NQ), (3, 4, HZ, NQ),
+        (2, W, NQ), (2, HZ, W), (HZ, W), (3, GC, W), (HZ, W), (3, HZ, NQ), (2, HZ, NQ), (2, GC, W),
+        (W, NQ), (R, R, SP, NQ), (HW, R, SP, W), (3, R, SP, NQ), (2, R, SP, W),
+        (SP, NQ), (HZ, W), (2, SP, W), (2, HZ, NQ), (2, HZ, NQ), (2, GC, W),
         (2, R, R, SP, NQ), (2, R - 1, SP, NQ), (2, SP, NQ), (2, GC, W),
     ]
+    hbm = pl.BlockSpec(memory_space=pl.ANY)
     whole = pl.pallas_call(
         functools.partial(kernel, R, C, W, planes),
         out_shape=jax.ShapeDtypeStruct((8, GC, W), f32),
-        in_specs=[vmem, pl.BlockSpec(memory_space=pl.ANY), vmem, vmem, smem],
+        in_specs=[hbm, hbm, hbm, hbm, smem],
         out_specs=vmem,
         scratch_shapes=[pltpu.VMEM(shape, f32) for shape in scratch]
+        + [pltpu.VMEM((W, W), jnp.bfloat16)] * 4
         + [pltpu.SemaphoreType.DMA((N_SEM,)), pltpu.SemaphoreType.DMA((N_SEM,))],
         compiler_params=pltpu.CompilerParams(
-            collective_id=0, has_side_effects=True, vmem_limit_bytes=24 * 2**20
+            collective_id=0, has_side_effects=True, vmem_limit_bytes=60 * 2**20
         ),
     )(region_inverse, factor_cols, parent_factor, diag_inverse, listed)
     return pl.pallas_call(

time: 85.5 us -> 78 us (0.912)
  local copies, waits for them, and re-layouts: 5.24 us -> 0.94 us
  Pallas kernels: 79 us -> 76.2 us
    unnamed x10 -> x2, local copies, waits for them, and re-layouts: 5.24 us -> 0.94 us
    pallas_call x1, Pallas kernels: 78.3 us -> 75.5 us  [shards(): pl.pallas_call(functools.partial(kernel, R, C, W, planes), out_shape=jax....]
where the time goes in v3:
time: 78 us; the launch traced here: 77.8 us
  Pallas kernels  76.2 us (98%)
  local copies, waits for them, and re-layouts  0.94 us (1%)
    pallas_call x1, Pallas kernels, shards(): pl.pallas_call(functools.partial(kernel, R, C, W, planes), out_shape=jax....  75.5 us

profile of v3, /device:TPU:1, one launch (start us, length us, event | category | flops | bytes accessed | tf_op | source)
XLA Modules:
  0.0 77.8 jit_solution(17926473475656795551)
XLA Ops:
  0.6 75.5 %shard_map.76.whole_ref = f32[8,16,512]{2,1,0:T(8,128)} custom-call(f32[512,128]{1,0:T(8,128)} %a_ref.1, f32[3,512,512]{2,1,0:T(8,128)} %f_ref.1, f32[2,16,512]{2,1,0:T(8,128)} %g_ref.1, f32[3,16,512]{2,1,0:T(8,128)} %d_ref.1, s32[3,8]{1,0:T(4,128)} %listed_ref.1), custom_call_target="tpu_custom_call" | custom-call | tf_op jit(solution)/shard_map/pallas_call | solution.py:593
  76.1 0.0 copy-start
  76.1 0.9 %copy-done = f32[8,16,512]{2,1,0:T(8,128)S(1)} copy-done((f32[8,16,512]{2,1,0:T(8,128)S(1)}, f32[8,16,512]{2,1,0:T(8,128)}, u32[]{:S(2)}) %copy-start) | copy-done | bytes 262168
  77.1 0.7 shard_map.77
Async XLA Ops:
  76.1 1.0 %copy-start = (f32[8,16,512]{2,1,0:T(8,128)S(1)}, f32[8,16,512]{2,1,0:T(8,128)}, u32[]{:S(2)}) copy-start(f32[8,16,512]{2,1,0:T(8,128)} %shard_map.76.whole_ref) | copy-start | bytes 786436

commit v4 on v3

--- a/solution.py
+++ b/solution.py
@@ -63,25 +63,44 @@
     HR = R // 2
     r = lax.axis_index("row")
     c = lax.axis_index("col")
-    z = c // Q
-    q = c % Q
-
-    def flip(row, place):
-        return 2 * ((place // 2 + row // HR) % 2) + place % 2
-
-    def at(row, k):
-        return (row // HR + k // HR) % 2 * HR + (row % HR + k % HR) % HR
-
-    n = flip(r, q)
-    partner = at(z, HR)
-    core = q % 2
-    sibling = q + 1 - 2 * core
-    across = (q + 2) % Q
-    n_cols = pl.ds(pl.multiple_of(n * NQ, NQ), NQ)
+
+    def wrap(value, size):
+        return jnp.where(value >= size, value - size, value)
+
+    z = lax.div(c, Q)
+    q = c - z * Q
+    half = lax.div(r, HR)
+    y = r - half * HR
+    pair = lax.div(q, 2)
+    core = q - pair * 2
+    z_half = lax.div(z, HR)
+    z_y = z - z_half * HR
+    kind = jnp.where(pair == half, 0, 1)
+    across = 2 * (1 - pair) + core
+    sibling = 2 * pair + 1 - core
+    diagonal = 2 * (1 - pair) + 1 - core
+    node = (q, sibling, across, diagonal)
+    n = 2 * kind + core
+    shares = (n, 2 * kind + 1 - core, 2 * (1 - kind) + core, 2 * (1 - kind) + 1 - core)
+    other_shares = (shares[2], shares[3], shares[0], shares[1])
+    ys = [wrap(y + k, HR) if k else y for k in range(HR)]
+    rows = [half * HR + v for v in ys] + [(1 - half) * HR + v for v in ys]
+    qs = [q] * HR + [across] * HR
+    zs = [wrap(z + k, R) if k else z for k in range(R)]
+    zc = [v * Q for v in zs]
+    base = zc[0]
+    zd = [zs[k] if k % HR == 0 else jnp.where(core == 0, zs[k], zs[R - k]) for k in range(R)]
+    far = half != z_half
+    place_of = wrap(y - z_y + HR, HR) + jnp.where(far, HR, 0)
+    partner = z + HR - 2 * HR * z_half
+
+    def span(i, size):
+        return pl.ds(pl.multiple_of(i * size, size), size)
 
     def piece(i):
-        return pl.ds(pl.multiple_of(i * HZ, HZ), HZ)
-
+        return span(i, HZ)
+
+    n_cols = span(n, NQ)
     my_rows = piece(z)
 
     def push(src, dst, s, row, col, k=0):
@@ -106,25 +125,28 @@
         pl.semaphore_signal(barrier, inc=1, device_id=(row, col), device_id_type=MESH)
 
     for k in range(1, R):
-        i = at(r, k)
-        greet(i, z * Q + flip(i, n))
+        greet(rows[k], base + qs[k])
     for k in range(1, R):
-        greet(r, (z + k) % R * Q + q)
+        greet(r, zc[k] + q)
     for k in range(1, Q):
-        greet(r, z * Q + (q + k) % Q)
-    for k, offset in OFFSET.items():
-        if offset:
-            @pl.when(at(z, k) == r)
-            def _():
-                greet(z, (z + offset) % R * Q + flip(z, n))
+        greet(r, base + node[k])
+    q_source = jnp.where(far, across, q)
+    for step in (1, -1):
+        ours = functools.reduce(
+            jnp.logical_or, [place_of == k for k, offset in OFFSET.items() if offset == step]
+        )
+
+        @pl.when(ours)
+        def _():
+            greet(z, zc[step % R] + q_source)
 
     near = z == r
-    above = z == (r + 1) % R
-    below = (z + 1) % R == r
-    a_cols = pl.ds(pl.multiple_of(q * NQ, NQ), NQ)
-    x_cols = pl.ds(pl.multiple_of(across * NQ, NQ), NQ)
-    n_rows = pl.ds(pl.multiple_of(q * GC, GC), GC)
-    g_rows = pl.ds(pl.multiple_of(c * GC, GC), GC)
+    above = zs[R - 1] == r
+    below = zs[1] == r
+    a_cols = span(q, NQ)
+    x_cols = span(across, NQ)
+    n_rows = span(q, GC)
+    g_rows = span(c, GC)
 
     def local(src, dst, s, k=0):
         pltpu.make_async_copy(src, dst, recv.at[BASE[s] + k]).start()
@@ -176,26 +198,20 @@
             for j in range(3):
                 for k, source in OFFSET.items():
                     if source == offset:
-                        i = at(r, k)
                         push(
-                            f_ref.at[j, piece(i), n_cols], fb.at[j, piece(i)], "FS",
-                            i, r * Q + flip(i, n), j,
+                            f_ref.at[j, piece(rows[k]), n_cols], fb.at[j, piece(rows[k])], "FS",
+                            rows[k], r * Q + qs[k], j,
                         )
                 if offset == 0:
                     push(
                         f_ref.at[j, piece(z), n_cols], fb.at[j, piece(z)], "FS",
-                        partner, z * Q + flip(partner, n), j,
+                        rows[HR], base + across, j,
                     )
 
     for k in range(1, Q):
-        other = (q + k) % Q
-        share = flip(r, other)
-        push(
-            g_ref.at[:, :, pl.ds(pl.multiple_of(share * NQ, NQ), NQ)], gc.at[:, g_rows], "G0",
-            r, z * Q + other,
-        )
-    push(a_ref, abuf.at[:, a_cols], "A", r, z * Q + across, 1)
-    push(a_ref, abuf.at[:, a_cols], "A", r, z * Q + sibling, 0)
+        push(g_ref.at[:, :, span(shares[k], NQ)], gc.at[:, g_rows], "G0", r, base + node[k])
+    push(a_ref, abuf.at[:, a_cols], "A", r, base + across, 1)
+    push(a_ref, abuf.at[:, a_cols], "A", r, base + sibling, 0)
 
     def forward(j):
         @pl.when(r != z)
@@ -209,38 +225,36 @@
                 arrived(fb.at[j, :HZ], "FS", j)
 
             for k in range(1, R):
-                i = at(r, k)
-
-                @pl.when(i != z)
+                @pl.when(rows[k] != z)
                 def _():
-                    push(fb.at[j, piece(r)], fb.at[j, piece(r)], "FA", i, z * Q + flip(i, n), j)
-
-                    @pl.when(r == partner)
-                    def _():
+                    push(fb.at[j, piece(r)], fb.at[j, piece(r)], "FA", rows[k], base + qs[k], j)
+
+            @pl.when(r == partner)
+            def _():
+                for k in range(1, R):
+                    if k != HR:
                         pltpu.make_async_remote_copy(
                             src_ref=fb.at[j, piece(z)], dst_ref=fb.at[j, piece(z)],
                             send_sem=send.at[BASE["FX"]], recv_sem=recv.at[BASE["FA"] + j],
-                            device_id=(i, z * Q + flip(i, n)), device_id_type=MESH,
+                            device_id=(rows[k], base + qs[k]), device_id_type=MESH,
                         ).start()
 
     def g_step(k):
         if k == 0:
             loaded(gc.at[:, g_rows], "LC")
             arrived(gc.at[:, : (Q - 1) * GC], "G0")
-        up = gc.at[:, piece((z - k) % R)]
-        down = gc.at[:, piece((z + k) % R)]
+        up = gc.at[:, piece(zs[-k % R])]
+        down = gc.at[:, piece(zs[k])]
         if k:
             arrived(up, "GP", k - 1)
-        push(up, up, "GP", r, (z + 1) % R * Q + q, k)
+        push(up, up, "GP", r, zc[1] + q, k)
         if k < R - 1 - HR:
             if k:
                 arrived(down, "GM", k - 1)
-            push(down, down, "GM", r, (z - 1) % R * Q + q, k)
-
-    s = 1 - 2 * core
+            push(down, down, "GM", r, zc[R - 1] + q, k)
 
     def along(k):
-        return (z + s * k) % R
+        return zd[k % R]
 
     def product(j):
         @pl.when(r == z)
@@ -275,25 +289,25 @@
 
     g_step(0)
     forward(0)
+    forward(1)
     g_step(1)
-    forward(1)
-    g_step(2)
     forward(2)
     arrived(abuf.at[:, x_cols], "A", 1)
-    push(abuf.at[:, x_cols], abuf.at[:, x_cols], "A", r, z * Q + sibling, 2)
+    push(abuf.at[:, x_cols], abuf.at[:, x_cols], "A", r, base + sibling, 2)
     loaded(abuf.at[:, a_cols], "LA")
     for k in range(1, Q):
-        push(g_ref, gn.at[:, n_rows], "GN", r, z * Q + (q + k) % Q)
-        push(d_ref.at[0], db.at[n_rows], "D", r, z * Q + (q + k) % Q)
-    g_step(3)
+        push(g_ref, gn.at[:, n_rows], "GN", r, base + node[k])
+        push(d_ref.at[0], db.at[n_rows], "D", r, base + node[k])
     arrived(abuf.at[:, a_cols], "A", 0)
     arrived(abuf.at[:, a_cols], "A", 2)
     ah[...], al[...] = halves(abuf[...])
     product(0)
+    g_step(2)
     product(1)
     relay(0)
     product(2)
     relay(1)
+    g_step(3)
 
     def summed(j):
         arrived(rb.at[j], "RB", j)
@@ -310,15 +324,15 @@
 
     yc[0] = -weight(0, r) * summed(0)
     for k in range(1, Q):
-        push(yc.at[0], y0n.at[:, n_cols], "Y0", r, z * Q + (q + k) % Q)
+        push(yc.at[0], y0n.at[:, n_cols], "Y0", r, base + node[k])
     for plane in planes[:3]:
         to_unit(0, plane)
     y0n[:, n_cols] = yc[0]
     relay(2)
     arrived(y0n.at[:, : (Q - 1) * NQ], "Y0")
     out_ref[0] = y0n[n_rows]
-    arrived(gc.at[:, piece((z - HR) % R)], "GP", HR - 1)
-    arrived(gc.at[:, piece((z + HR - 1) % R)], "GM", HR - 2)
+    arrived(gc.at[:, piece(zs[HR])], "GP", HR - 1)
+    arrived(gc.at[:, piece(zs[HR - 1])], "GM", HR - 2)
     for j in (1, 2):
         xc[j - 1] = mm(y0n[...], gc[j - 1])
 
@@ -326,10 +340,8 @@
         yc[j] = -weight(j, r) * (summed(j) + xc[j - 1])
         to_unit(j, planes[2 + j])
         for k in range(1, Q):
-            other = (q + k) % Q
             push(
-                yc.at[j, pl.ds(pl.multiple_of(other * GC, GC), GC)], yo.at[j - 1, :, n_cols],
-                "YO", r, z * Q + other,
+                yc.at[j, span(node[k], GC)], yo.at[j - 1, :, n_cols], "YO", r, base + node[k]
             )
         yo[j - 1, :, n_cols] = yc[j, n_rows]
 
@@ -340,11 +352,12 @@
             tp[...] = mm3(fh[...], fl[...], yu[...]).reshape(R, R, SP, NQ)
             zr[place, 0] = tp[z, r]
 
-            @pl.loop(1, R * R)
-            def _(t):
-                i = at(r, t // R)
-                dest = (z + t % R) % R
-                push(tp.at[dest, i], zr.at[place, t // R], "ZM", i, dest * Q + flip(i, n), place)
+            for m in range(R):
+                for k in range(R):
+                    if m or k:
+                        push(
+                            tp.at[zs[m], rows[k]], zr.at[place, k], "ZM", rows[k], zc[m] + qs[k], place
+                        )
 
     def cross_sum(unit, child):
         @pl.when(z == planes[unit])
@@ -354,21 +367,22 @@
             total = dot(y_hi, fh[...]) + (dot(y_hi, fl[...]) + dot(y_lo, fh[...]))
             tpw[...] = (total * weight(1 + child, r)).reshape(HW, R, SP, W)
 
-            @pl.loop(0, R * HW)
-            def _(t):
-                i = at(r, t // HW)
-                dest = n * HW + t % HW
-                own = (t < HW) & (dest == z)
-
-                @pl.when(own)
-                def _():
-                    wr[child, 0] = tpw[t % HW, r]
-
-                @pl.when(jnp.logical_not(own))
-                def _():
-                    push(
-                        tpw.at[t % HW, i], wr.at[child, t // HW], "WM", i, dest * Q + flip(i, n), child
-                    )
+            for h in range(HW):
+                dest = n * HW + h
+                for k in range(R):
+                    if k:
+                        push(
+                            tpw.at[h, rows[k]], wr.at[child, k], "WM", rows[k], dest * Q + qs[k], child
+                        )
+                        continue
+
+                    @pl.when(dest == z)
+                    def _():
+                        wr[child, 0] = tpw[h, r]
+
+                    @pl.when(dest != z)
+                    def _():
+                        push(tpw.at[h, r], wr.at[child, 0], "WM", r, dest * Q + q, child)
 
     def added(place, plane):
         @pl.when(z == plane)
@@ -389,19 +403,16 @@
     rows_sum(3, 1, 1)
     rows_sum(4, 2, 2)
 
-    s_rows = pl.ds(pl.multiple_of(r * SP, SP), SP)
-    flat = r * Q + q
-
+    s_rows = span(r, SP)
     zm[...] = added(0, planes[0])
-
-    @pl.loop(1, C)
-    def _(k):
-        other = (flat + k) % C
-        push(zm, zb.at[s_rows, n_cols], "ZB", other // Q, z * Q + other % Q)
+    for k in range(R):
+        for w in range(Q):
+            if k or w:
+                push(zm, zb.at[s_rows, n_cols], "ZB", rows[k], base + node[w])
 
     zb[s_rows, n_cols] = zm[...]
 
-    holds_w = z // HW == n
+    holds_w = lax.div(z, HW) == n
 
     @pl.when(holds_w)
     def _():
@@ -416,14 +427,14 @@
 
             wm[child] = functools.reduce(jnp.add, [wr[child, k] for k in range(R)])
 
-            @pl.loop(1, C)
-            def _(k):
-                other = (flat + k) % C
-                share = flip(other // Q, other % Q)
-                push(
-                    wm.at[child, :, pl.ds(pl.multiple_of(share * NQ, NQ), NQ)],
-                    wb.at[child, s_rows], "WB", other // Q, z * Q + other % Q, child,
-                )
+            for k in range(R):
+                for w in range(Q):
+                    if k or w:
+                        share = (shares if k < HR else other_shares)[w]
+                        push(
+                            wm.at[child, :, span(share, NQ)], wb.at[child, s_rows], "WB",
+                            rows[k], base + node[w], child,
+                        )
 
             wb[child, s_rows] = wm[child, :, n_cols]
 
@@ -447,18 +458,15 @@
         eb[child] = wb[child] + mm(zb[...], gc[child])
         ge[child] = mm_t(gn[child], eb[child]).reshape(R, R, SP, NQ)
         for k in range(1, R):
-            dest = (z + k) % R
-            push(ge.at[child, dest, r], gz.at[child, R - 1 - k], "GZ", r, dest * Q + q, child)
+            push(ge.at[child, zs[k], r], gz.at[child, R - 1 - k], "GZ", r, zc[k] + q, child)
         for k in range(1, Q):
-            other = (q + k) % Q
             push(
-                eb.at[child, pl.ds(pl.multiple_of(other * GC, GC), GC)], uo.at[child, :, n_cols],
-                "UO", r, z * Q + other,
+                eb.at[child, span(node[k], GC)], uo.at[child, :, n_cols], "UO", r, base + node[k],
             )
         uo[child, :, n_cols] = eb[child, n_rows]
 
-    o_rows = pl.ds(pl.multiple_of(r % (R // Q) * SP, SP), SP)
-    o_place = r // (R // Q)
+    o_place = lax.div(r, R // Q)
+    o_rows = span(r - o_place * (R // Q), SP)
     for child in range(2):
         share = added(1 + child, planes[3 + child])
         arrived(gz.at[child], "GZ", child)
@@ -468,7 +476,7 @@
         zp[child] = total
         for k in range(1, R):
             push(
-                zp.at[child], zo.at[child, o_rows, n_cols], "ZO", (r + k) % R, z * Q + o_place, child
+                zp.at[child], zo.at[child, o_rows, n_cols], "ZO", rows[k], base + o_place, child
             )
 
         @pl.when(q == o_place)
@@ -477,7 +485,7 @@
 
         @pl.when(q != o_place)
         def _():
-            push(zp.at[child], zo.at[child, o_rows, n_cols], "ZO", r, z * Q + o_place, child)
+            push(zp.at[child], zo.at[child, o_rows, n_cols], "ZO", r, base + o_place, child)
 
     arrived(yo.at[:, :, : (Q - 1) * NQ], "YO")
     out_ref[1:3] = yo[...]

time: 78 us -> 77.6 us (level)
  no operation moved by 1% of the time
where the time goes in v4:
time: 77.6 us; the launch traced here: 77.4 us
  Pallas kernels  75.8 us (98%)
  local copies, waits for them, and re-layouts  0.94 us (1%)
    pallas_call x1, Pallas kernels, shards(): pl.pallas_call(functools.partial(kernel, R, C, W, planes), out_shape=jax....  75.1 us

profile of v4, /device:TPU:1, one launch (start us, length us, event | category | flops | bytes accessed | tf_op | source)
XLA Modules:
  0.0 77.4 jit_solution(2878613451340926674)
XLA Ops:
  0.6 75.1 %shard_map.76.whole_ref = f32[8,16,512]{2,1,0:T(8,128)} custom-call(f32[512,128]{1,0:T(8,128)} %a_ref.1, f32[3,512,512]{2,1,0:T(8,128)} %f_ref.1, f32[2,16,512]{2,1,0:T(8,128)} %g_ref.1, f32[3,16,512]{2,1,0:T(8,128)} %d_ref.1, s32[3,8]{1,0:T(4,128)} %listed_ref.1), custom_call_target="tpu_custom_call" | custom-call | tf_op jit(solution)/shard_map/pallas_call | solution.py:601
  75.8 0.0 copy-start
  75.8 0.9 %copy-done = f32[8,16,512]{2,1,0:T(8,128)S(1)} copy-done((f32[8,16,512]{2,1,0:T(8,128)S(1)}, f32[8,16,512]{2,1,0:T(8,128)}, u32[]{:S(2)}) %copy-start) | copy-done | bytes 262168
  76.7 0.7 shard_map.77
Async XLA Ops:
  75.8 1.0 %copy-start = (f32[8,16,512]{2,1,0:T(8,128)S(1)}, f32[8,16,512]{2,1,0:T(8,128)}, u32[]{:S(2)}) copy-start(f32[8,16,512]{2,1,0:T(8,128)} %shard_map.76.whole_ref) | copy-start | bytes 786436

commit v5 on v4

--- a/solution.py
+++ b/solution.py
@@ -19,9 +19,6 @@
 for _name, _size in SIZES.items():
     BASE[_name] = N_SEM
     N_SEM += _size
-
-OFFSET = {1: 0, 3: 0, 4: 0, 2: -1, 7: -1, 5: 1, 6: 1}
-
 
 def halves(x):
     hi = x.astype(jnp.bfloat16)
@@ -74,7 +71,6 @@
     pair = lax.div(q, 2)
     core = q - pair * 2
     z_half = lax.div(z, HR)
-    z_y = z - z_half * HR
     kind = jnp.where(pair == half, 0, 1)
     across = 2 * (1 - pair) + core
     sibling = 2 * pair + 1 - core
@@ -90,8 +86,6 @@
     zc = [v * Q for v in zs]
     base = zc[0]
     zd = [zs[k] if k % HR == 0 else jnp.where(core == 0, zs[k], zs[R - k]) for k in range(R)]
-    far = half != z_half
-    place_of = wrap(y - z_y + HR, HR) + jnp.where(far, HR, 0)
     partner = z + HR - 2 * HR * z_half
 
     def span(i, size):
@@ -130,19 +124,7 @@
         greet(r, zc[k] + q)
     for k in range(1, Q):
         greet(r, base + node[k])
-    q_source = jnp.where(far, across, q)
-    for step in (1, -1):
-        ours = functools.reduce(
-            jnp.logical_or, [place_of == k for k, offset in OFFSET.items() if offset == step]
-        )
-
-        @pl.when(ours)
-        def _():
-            greet(z, zc[step % R] + q_source)
-
     near = z == r
-    above = zs[R - 1] == r
-    below = zs[1] == r
     a_cols = span(q, NQ)
     x_cols = span(across, NQ)
     n_rows = span(q, GC)
@@ -154,19 +136,19 @@
     def loaded(view, s, k=0):
         pltpu.make_async_copy(view, view, recv.at[BASE[s] + k]).wait()
 
-    for unit, member in enumerate((0, 1, 2, 1, 2)):
-        @pl.when(z == planes[unit])
-        def _():
-            local(f_ref.at[member], fv, "FV")
-
-    local(g_ref.at[:, :, n_cols], gc.at[:, g_rows], "LC")
-    local(a_ref, abuf.at[:, a_cols], "LA")
-
     @pl.when(near)
     def _():
         for j in range(3):
             local(f_ref.at[j, :, n_cols], fb.at[j], "FB", j)
 
+    local(a_ref, abuf.at[:, a_cols], "LA")
+    local(g_ref.at[:, :, n_cols], gc.at[:, g_rows], "LC")
+    for unit, member in enumerate((0, 1, 2, 1, 2)):
+        @pl.when(z == planes[unit])
+        def _():
+            local(f_ref.at[member], fv, "FV")
+
+
     local(g_ref, gn.at[:, n_rows], "LG")
     local(d_ref, dv, "LD")
     in_cols = functools.reduce(jnp.logical_or, [z == planes[unit] for unit in (0, 3, 4)])
@@ -182,36 +164,23 @@
         loaded(fv, "FV")
         fh[...], fl[...] = halves(fv[...])
 
-    peers = 2 * (R - 1) + Q - 1
-
-    @pl.when(above | below)
+    pl.semaphore_wait(barrier, 2 * (R - 1) + Q - 1)
+
+    @pl.when(near)
     def _():
-        pl.semaphore_wait(barrier, peers + 2)
-
-    @pl.when(jnp.logical_not(above | below))
-    def _():
-        pl.semaphore_wait(barrier, peers)
-
-    for offset, here in ((0, near), (1, above), (-1, below)):
-        @pl.when(here)
-        def _():
-            for j in range(3):
-                for k, source in OFFSET.items():
-                    if source == offset:
-                        push(
-                            f_ref.at[j, piece(rows[k]), n_cols], fb.at[j, piece(rows[k])], "FS",
-                            rows[k], r * Q + qs[k], j,
-                        )
-                if offset == 0:
-                    push(
-                        f_ref.at[j, piece(z), n_cols], fb.at[j, piece(z)], "FS",
-                        rows[HR], base + across, j,
-                    )
+        for j in range(3):
+            loaded(fb.at[j], "FB", j)
+            for k in range(1, R):
+                push(
+                    fb.at[j, piece(rows[k])], fb.at[j, piece(rows[k])], "FS", rows[k], base + qs[k], j
+                )
+            push(fb.at[j, piece(z)], fb.at[j, piece(z)], "FS", rows[HR], base + across, j)
 
     for k in range(1, Q):
         push(g_ref.at[:, :, span(shares[k], NQ)], gc.at[:, g_rows], "G0", r, base + node[k])
-    push(a_ref, abuf.at[:, a_cols], "A", r, base + across, 1)
-    push(a_ref, abuf.at[:, a_cols], "A", r, base + sibling, 0)
+    loaded(abuf.at[:, a_cols], "LA")
+    push(abuf.at[:, a_cols], abuf.at[:, a_cols], "A", r, base + across, 1)
+    push(abuf.at[:, a_cols], abuf.at[:, a_cols], "A", r, base + sibling, 0)
 
     def forward(j):
         @pl.when(r != z)
@@ -257,10 +226,6 @@
         return zd[k % R]
 
     def product(j):
-        @pl.when(r == z)
-        def _():
-            loaded(fb.at[j], "FB", j)
-
         @pl.when((r != z) & (r != partner))
         def _():
             arrived(fb.at[j, : (R - 1) * HZ], "FA", j)
@@ -294,7 +259,6 @@
     forward(2)
     arrived(abuf.at[:, x_cols], "A", 1)
     push(abuf.at[:, x_cols], abuf.at[:, x_cols], "A", r, base + sibling, 2)
-    loaded(abuf.at[:, a_cols], "LA")
     for k in range(1, Q):
         push(g_ref, gn.at[:, n_rows], "GN", r, base + node[k])
         push(d_ref.at[0], db.at[n_rows], "D", r, base + node[k])
@@ -518,11 +482,7 @@
     for j in range(3):
         @pl.when(near)
         def _():
-            sent(fb.at[j, : 4 * HZ], "FS", j)
-
-        @pl.when(above | below)
-        def _():
-            sent(fb.at[j, : 2 * HZ], "FS", j)
+            sent(fb.at[j], "FS", j)
 
         @pl.when(r != z)
         def _():

time: 77.6 us -> 74.6 us (0.961)
  Pallas kernels: 75.8 us -> 72.8 us
    pallas_call x1, Pallas kernels: 75.1 us -> 72.1 us  [shards(): pl.pallas_call(functools.partial(kernel, R, C, W, planes), out_shape=jax....]
where the time goes in v5:
time: 74.6 us; the launch traced here: 74.4 us
  Pallas kernels  72.8 us (98%)
  local copies, waits for them, and re-layouts  0.94 us (1%)
    pallas_call x1, Pallas kernels, shards(): pl.pallas_call(functools.partial(kernel, R, C, W, planes), out_shape=jax....  72.1 us

profile of v5, /device:TPU:1, one launch (start us, length us, event | category | flops | bytes accessed | tf_op | source)
XLA Modules:
  0.0 74.4 jit_solution(11712833882364281230)
XLA Ops:
  0.6 72.1 %shard_map.76.whole_ref = f32[8,16,512]{2,1,0:T(8,128)} custom-call(f32[512,128]{1,0:T(8,128)} %a_ref.1, f32[3,512,512]{2,1,0:T(8,128)} %f_ref.1, f32[2,16,512]{2,1,0:T(8,128)} %g_ref.1, f32[3,16,512]{2,1,0:T(8,128)} %d_ref.1, s32[3,8]{1,0:T(4,128)} %listed_ref.1), custom_call_target="tpu_custom_call" | custom-call | tf_op jit(solution)/shard_map/pallas_call | solution.py:561
  72.8 0.0 copy-start
  72.8 0.9 %copy-done = f32[8,16,512]{2,1,0:T(8,128)S(1)} copy-done((f32[8,16,512]{2,1,0:T(8,128)S(1)}, f32[8,16,512]{2,1,0:T(8,128)}, u32[]{:S(2)}) %copy-start) | copy-done | bytes 262168
  73.7 0.7 shard_map.77
Async XLA Ops:
  72.8 1.0 %copy-start = (f32[8,16,512]{2,1,0:T(8,128)S(1)}, f32[8,16,512]{2,1,0:T(8,128)}, u32[]{:S(2)}) copy-start(f32[8,16,512]{2,1,0:T(8,128)} %shard_map.76.whole_ref) | copy-start | bytes 786436

commit v6 on v5

--- a/solution.py
+++ b/solution.py
@@ -11,7 +11,7 @@
 HIGH = lax.Precision.HIGHEST
 
 SIZES = dict(
-    A=3, FS=3, FA=3, FX=1, GN=1, G0=1, D=1, GP=4, GM=3, X=3, RB=3, Y0=1, YO=1, YU=3, ZM=3, ZB=1, WM=2,
+    A=3, FS=3, FA=3, FX=1, GN=1, G0=1, D=1, GP=1, X=3, RB=3, Y0=1, YO=1, YU=3, ZM=3, ZB=1, WM=2,
     WB=2, UO=1, GZ=2, ZO=2, FB=3, FV=1, LA=1, LG=1, LC=1, LD=1,
 )
 BASE = {}
@@ -175,6 +175,8 @@
                     fb.at[j, piece(rows[k])], fb.at[j, piece(rows[k])], "FS", rows[k], base + qs[k], j
                 )
             push(fb.at[j, piece(z)], fb.at[j, piece(z)], "FS", rows[HR], base + across, j)
+            for k in range(1, HR):
+                push(fb.at[j, piece(z)], fb.at[j, piece(z)], "FA", rows[k], base + q, j)
 
     for k in range(1, Q):
         push(g_ref.at[:, :, span(shares[k], NQ)], gc.at[:, g_rows], "G0", r, base + node[k])
@@ -200,27 +202,18 @@
 
             @pl.when(r == partner)
             def _():
-                for k in range(1, R):
-                    if k != HR:
-                        pltpu.make_async_remote_copy(
-                            src_ref=fb.at[j, piece(z)], dst_ref=fb.at[j, piece(z)],
-                            send_sem=send.at[BASE["FX"]], recv_sem=recv.at[BASE["FA"] + j],
-                            device_id=(rows[k], base + qs[k]), device_id_type=MESH,
-                        ).start()
-
-    def g_step(k):
-        if k == 0:
-            loaded(gc.at[:, g_rows], "LC")
-            arrived(gc.at[:, : (Q - 1) * GC], "G0")
-        up = gc.at[:, piece(zs[-k % R])]
-        down = gc.at[:, piece(zs[k])]
-        if k:
-            arrived(up, "GP", k - 1)
-        push(up, up, "GP", r, zc[1] + q, k)
-        if k < R - 1 - HR:
-            if k:
-                arrived(down, "GM", k - 1)
-            push(down, down, "GM", r, zc[R - 1] + q, k)
+                for k in range(1, HR):
+                    pltpu.make_async_remote_copy(
+                        src_ref=fb.at[j, piece(z)], dst_ref=fb.at[j, piece(z)],
+                        send_sem=send.at[BASE["FX"]], recv_sem=recv.at[BASE["FA"] + j],
+                        device_id=(rows[k], base + q), device_id_type=MESH,
+                    ).start()
+
+    def share_columns():
+        loaded(gc.at[:, g_rows], "LC")
+        arrived(gc.at[:, : (Q - 1) * GC], "G0")
+        for k in range(1, R):
+            push(gc.at[:, my_rows], gc.at[:, my_rows], "GP", r, zc[k] + q)
 
     def along(k):
         return zd[k % R]
@@ -252,10 +245,9 @@
         push(rl.at[j, 0], rb.at[j, 2], "RB", r, along(2) * Q + q, j)
         push(rl.at[j, 1], rb.at[j, 3], "RB", r, along(-2) * Q + q, j)
 
-    g_step(0)
+    share_columns()
     forward(0)
     forward(1)
-    g_step(1)
     forward(2)
     arrived(abuf.at[:, x_cols], "A", 1)
     push(abuf.at[:, x_cols], abuf.at[:, x_cols], "A", r, base + sibling, 2)
@@ -266,12 +258,9 @@
     arrived(abuf.at[:, a_cols], "A", 2)
     ah[...], al[...] = halves(abuf[...])
     product(0)
-    g_step(2)
     product(1)
     relay(0)
-    product(2)
     relay(1)
-    g_step(3)
 
     def summed(j):
         arrived(rb.at[j], "RB", j)
@@ -292,11 +281,10 @@
     for plane in planes[:3]:
         to_unit(0, plane)
     y0n[:, n_cols] = yc[0]
-    relay(2)
+    product(2)
     arrived(y0n.at[:, : (Q - 1) * NQ], "Y0")
     out_ref[0] = y0n[n_rows]
-    arrived(gc.at[:, piece(zs[HR])], "GP", HR - 1)
-    arrived(gc.at[:, piece(zs[HR - 1])], "GM", HR - 2)
+    arrived(gc.at[:, : (R - 1) * HZ], "GP")
     for j in (1, 2):
         xc[j - 1] = mm(y0n[...], gc[j - 1])
 
@@ -359,6 +347,7 @@
 
         return functools.reduce(jnp.add, [zr[place, k] for k in range(R)])
 
+    relay(2)
     rows_sum(0, 0, 0)
     cross_sum(1, 0)
     cross_sum(2, 1)
@@ -469,10 +458,7 @@
     for k in range(3):
         sent(abuf.at[:, a_cols], "A", k)
     sent(gc.at[:, : (Q - 1) * GC], "G0")
-    for k in range(HR):
-        sent(gc.at[:, my_rows], "GP", k)
-    for k in range(R - 1 - HR):
-        sent(gc.at[:, my_rows], "GM", k)
+    sent(gc.at[:, : (R - 1) * HZ], "GP")
     sent(gn.at[:, : (Q - 1) * GC], "GN")
     sent(db.at[: (Q - 1) * GC], "D")
     sent(y0n.at[:, : (Q - 1) * NQ], "Y0")
@@ -483,6 +469,7 @@
         @pl.when(near)
         def _():
             sent(fb.at[j], "FS", j)
+            sent(fb.at[j, : (HR - 1) * HZ], "FA", j)
 
         @pl.when(r != z)
         def _():
@@ -493,7 +480,7 @@
 
     @pl.when(r == partner)
     def _():
-        sent(fb.at[:, : (R - 2) * HZ], "FX")
+        sent(fb.at[:, : (HR - 1) * HZ], "FX")
 
     for j in range(3):
         targets = planes[:3] if j == 0 else planes[2 + j : 3 + j]

time: 74.6 us -> 72.4 us (0.971)
  Pallas kernels: 72.8 us -> 70.7 us
    pallas_call x1, Pallas kernels: 72.1 us -> 70 us  [shards(): pl.pallas_call(functools.partial(kernel, R, C, W, planes), out_shape=jax....]
where the time goes in v6:
time: 72.4 us; the launch traced here: 72.3 us
  Pallas kernels  70.7 us (98%)
  local copies, waits for them, and re-layouts  0.94 us (1%)
    pallas_call x1, Pallas kernels, shards(): pl.pallas_call(functools.partial(kernel, R, C, W, planes), out_shape=jax....  70 us

profile of v6, /device:TPU:1, one launch (start us, length us, event | category | flops | bytes accessed | tf_op | source)
XLA Modules:
  0.0 72.3 jit_solution(10966408294762496592)
XLA Ops:
  0.6 70.0 %shard_map.76.whole_ref = f32[8,16,512]{2,1,0:T(8,128)} custom-call(f32[512,128]{1,0:T(8,128)} %a_ref.1, f32[3,512,512]{2,1,0:T(8,128)} %f_ref.1, f32[2,16,512]{2,1,0:T(8,128)} %g_ref.1, f32[3,16,512]{2,1,0:T(8,128)} %d_ref.1, s32[3,8]{1,0:T(4,128)} %listed_ref.1), custom_call_target="tpu_custom_call" | custom-call | tf_op jit(solution)/shard_map/pallas_call | solution.py:548
  70.6 0.0 copy-start
  70.6 0.9 %copy-done = f32[8,16,512]{2,1,0:T(8,128)S(1)} copy-done((f32[8,16,512]{2,1,0:T(8,128)S(1)}, f32[8,16,512]{2,1,0:T(8,128)}, u32[]{:S(2)}) %copy-start) | copy-done | bytes 262168
  71.6 0.7 shard_map.77
Async XLA Ops:
  70.6 1.0 %copy-start = (f32[8,16,512]{2,1,0:T(8,128)S(1)}, f32[8,16,512]{2,1,0:T(8,128)}, u32[]{:S(2)}) copy-start(f32[8,16,512]{2,1,0:T(8,128)} %shard_map.76.whole_ref) | copy-start | bytes 786436

commit v7 on v6

--- a/solution.py
+++ b/solution.py
@@ -564,16 +564,23 @@
             jax.ShapeDtypeStruct((3, GC, W), f32),
             jax.ShapeDtypeStruct((2, GC, W), f32),
         ),
-        in_specs=[vmem],
+        in_specs=[hbm],
         out_specs=(vmem, vmem, vmem),
-        compiler_params=pltpu.CompilerParams(vmem_limit_bytes=4 * 2**20),
+        scratch_shapes=[pltpu.SemaphoreType.DMA((3,))],
+        compiler_params=pltpu.CompilerParams(vmem_limit_bytes=60 * 2**20),
     )(whole)
 
 
-def split(whole_ref, col_ref, diag_ref, par_ref):
-    col_ref[...] = whole_ref[0:3]
-    diag_ref[...] = whole_ref[3:6]
-    par_ref[...] = whole_ref[6:8]
+def split(whole_ref, col_ref, diag_ref, par_ref, sems):
+    parts = ((0, 3, col_ref), (3, 6, diag_ref), (6, 8, par_ref))
+    copies = [
+        pltpu.make_async_copy(whole_ref.at[first:last], ref, sems.at[k])
+        for k, (first, last, ref) in enumerate(parts)
+    ]
+    for copy in copies:
+        copy.start()
+    for copy in copies:
+        copy.wait()
 
 
 def solution(mesh):

time: 72.4 us -> 72.5 us (level)
  local copies, waits for them, and re-layouts: 0.94 us -> 0 us
  Pallas kernels: 70.7 us -> 71.6 us
    pallas_call x1, Pallas kernels: 0.71 us -> 1.66 us  [shards(): pl.pallas_call(split, out_shape=(jax.ShapeDtypeStruct((3, GC, W), f32), j...]
    unnamed x2 -> x0, local copies, waits for them, and re-layouts: 0.94 us -> none
where the time goes in v7:
time: 72.5 us; the launch traced here: 72.3 us
  Pallas kernels  71.6 us (99%)
    pallas_call x1, Pallas kernels, shards(): pl.pallas_call(functools.partial(kernel, R, C, W, planes), out_shape=jax....  70 us
    pallas_call x1, Pallas kernels, shards(): pl.pallas_call(split, out_shape=(jax.ShapeDtypeStruct((3, GC, W), f32), j...  1.66 us

profile of v7, /device:TPU:1, one launch (start us, length us, event | category | flops | bytes accessed | tf_op | source)
XLA Modules:
  0.0 72.3 jit_solution(9412571333589471831)
XLA Ops:
  0.6 70.0 %shard_map.76.whole_ref = f32[8,16,512]{2,1,0:T(8,128)} custom-call(f32[512,128]{1,0:T(8,128)} %a_ref.1, f32[3,512,512]{2,1,0:T(8,128)} %f_ref.1, f32[2,16,512]{2,1,0:T(8,128)} %g_ref.1, f32[3,16,512]{2,1,0:T(8,128)} %d_ref.1, s32[3,8]{1,0:T(4,128)} %listed_ref.1), custom_call_target="tpu_custom_call" | custom-call | tf_op jit(solution)/shard_map/pallas_call | solution.py:548
  70.6 1.7 %shard_map.77 = (f32[3,16,512]{2,1,0:T(8,128)}, f32[3,16,512]{2,1,0:T(8,128)}, f32[2,16,512]{2,1,0:T(8,128)}) custom-call(f32[8,16,512]{2,1,0:T(8,128)} %shard_map.76.whole_ref), custom_call_target="tpu_custom_call" | custom-call | tf_op jit(solution)/shard_map/pallas_call | solution.py:560
